TPU v7x, 32 devices: a whole 2x2x4 slice. The times are simulated.
32 devices in a mesh: dx: 4 (over y, x), dy: 8 (over z, core).
Axes of the slice: x: 2, y: 2, z: 4, core: 2. Of those that a mesh axis runs over, the one named last changes fastest.
Arguments:
- fine_nodes: bfloat16 [128, 128, 512], P('dx', 'dy'), may hold values from -6 to 6
- fine_edges: bfloat16 [6, 128, 128, 512], P(None, 'dx', 'dy'), may hold values from -6 to 6
- fine_links: int32 [6, 128, 128], P(None, 'dx', 'dy'), may hold values from 0 to 48
- mid_nodes: bfloat16 [32, 32, 512], P('dx', 'dy'), may hold values from -6 to 6
- mid_edges: bfloat16 [6, 32, 32, 512], P(None, 'dx', 'dy'), may hold values from -6 to 6
- mid_links: int32 [6, 32, 32], P(None, 'dx', 'dy'), may hold values from 0 to 8
- coarse_nodes: bfloat16 [8, 8, 512], replicated, may hold values from -6 to 6
- coarse_edges: bfloat16 [6, 8, 8, 512], replicated, may hold values from -6 to 6
- coarse_links: int32 [6, 8, 8], replicated, may hold values from 0 to 63
- edge_self: bfloat16 [1, 512, 1536], replicated, may hold values from -0.25 to 0.25
- edge_sender: bfloat16 [1, 512, 1536], replicated, may hold values from -0.25 to 0.25
- edge_receiver: bfloat16 [1, 512, 1536], replicated, may hold values from -0.25 to 0.25
- edge_bias: float32 [1, 1536], replicated, may hold values from -6 to 6
- edge_output: bfloat16 [1, 1536, 512], replicated, may hold values from -0.15625 to 0.15625
- edge_gain: float32 [1, 512], replicated, may hold values from 0.1 to 1.9
- edge_shift: float32 [1, 512], replicated, may hold values from -3 to 3
- node_self: bfloat16 [1, 512, 1536], replicated, may hold values from -0.25 to 0.25
- node_summed: bfloat16 [1, 512, 1536], replicated, may hold values from -0.109375 to 0.109375
- node_bias: float32 [1, 1536], replicated, may hold values from -6 to 6
- node_output: bfloat16 [1, 1536, 512], replicated, may hold values from -0.15625 to 0.15625
- node_gain: float32 [1, 512], replicated, may hold values from 0.1 to 1.9
- node_shift: float32 [1, 512], replicated, may hold values from -3 to 3
- prolongation: bfloat16 [1, 512, 512], replicated, may hold values from -0.25 to 0.25
- pooling: bfloat16 [1, 512, 512], replicated, may hold values from -0.25 to 0.25
Outputs:
- fine_out: bfloat16 [128, 128, 512], P('dx', 'dy')
- fine_edges_out: bfloat16 [6, 128, 128, 512], P(None, 'dx', 'dy')
- mid_out: bfloat16 [32, 32, 512], P('dx', 'dy')
- mid_edges_out: bfloat16 [6, 32, 32, 512], P(None, 'dx', 'dy')
- coarse_out: bfloat16 [8, 8, 512], replicated
- coarse_edges_out: bfloat16 [6, 8, 8, 512], replicated
Inputs may be any that keep to these rules, and one draw needn't show every extreme that they name: `fine_links`: code q names the sender at offset (q // 7 - 3, q % 7 - 3) from the receiver. `mid_links`: code q names the sender at offset (q // 3 - 1, q % 3 - 1) from the receiver.
All inputs are finite; a program needn't handle non-finite values.
Results may differ from a plain program's by a relative error of at most 0.012.
Values may be sent and summed in bfloat16 or wider, within the bound.
A program may use at most 128 MiB of HBM per device.

v0:
```python
import jax
import jax.numpy as jnp
from jax import lax
from jax.sharding import PartitionSpec as P

FINE_REACH = 3
MID_REACH = 1


epsilon = 1e-05


def with_halo(value, sides, width):
    for axis, dim in sides:
        count, length = (lax.axis_size(axis), value.shape[dim])
        up = [(i, (i + 1) % count) for i in range(count)]
        down = [(j, i) for i, j in up]
        last = lax.slice_in_dim(value, length - width, length, axis=dim)
        leading = lax.slice_in_dim(value, 0, width, axis=dim)
        before = lax.ppermute(last, axis, up)
        after = lax.ppermute(leading, axis, down)
        value = jnp.concatenate([before, value, after], axis=dim)
    return value


def normalize(values, gain_term, shift_term):
    average = jnp.mean(values, axis=-1, keepdims=True)
    centred = values - average
    variance = jnp.mean(centred * centred, axis=-1, keepdims=True)
    return centred * lax.rsqrt(variance + epsilon) * gain_term + shift_term


def level_update(nodes, edges, sender_terms, senders, weights):
    (
        self_matrix,
        receiver_matrix,
        edge_bias,
        edge_output,
        edge_gain,
        edge_shift,
        node_self,
        node_summed,
        node_bias,
        node_output,
        node_gain,
        node_shift,
    ) = weights
    fanout, height, breadth, feature = edges.shape
    places = height * breadth
    flat_nodes = nodes.reshape(places, feature)
    flat_edges = edges.reshape(fanout * places, feature)
    receiver = jnp.dot(flat_nodes, receiver_matrix, preferred_element_type=jnp.float32) + edge_bias
    latent = jnp.dot(flat_edges, self_matrix, preferred_element_type=jnp.float32).reshape(
        fanout, places, -1
    )
    latent = (
        latent + jnp.take(sender_terms, senders.reshape(fanout, places), axis=0) + receiver[None]
    )
    hidden = jax.nn.silu(latent).astype(jnp.bfloat16).reshape(fanout * places, -1)
    message = jnp.dot(hidden, edge_output, preferred_element_type=jnp.float32)
    new_edges = (flat_edges.astype(jnp.float32) + normalize(message, edge_gain, edge_shift)).astype(
        jnp.bfloat16
    )
    new_edges = new_edges.reshape(fanout, places, feature)
    summed = jnp.sum(new_edges.astype(jnp.float32), axis=0).astype(jnp.bfloat16)
    node_hidden = jnp.dot(flat_nodes, node_self, preferred_element_type=jnp.float32)
    node_hidden = (
        node_hidden + jnp.dot(summed, node_summed, preferred_element_type=jnp.float32) + node_bias
    )
    node_hidden = jax.nn.silu(node_hidden).astype(jnp.bfloat16)
    node_message = jnp.dot(node_hidden, node_output, preferred_element_type=jnp.float32)
    new_nodes = (
        flat_nodes.astype(jnp.float32) + normalize(node_message, node_gain, node_shift)
    ).astype(jnp.bfloat16)
    return (
        new_nodes.reshape(height, breadth, feature),
        new_edges.reshape(fanout, height, breadth, feature),
    )


def offset_index(link_codes, reach_cells, padded_breadth):
    window_span = 2 * reach_cells + 1
    row_place = lax.broadcasted_iota(jnp.int32, link_codes.shape, 1)
    col_place = lax.broadcasted_iota(jnp.int32, link_codes.shape, 2)
    return (
        (row_place + link_codes // window_span) * padded_breadth
        + col_place
        + link_codes % window_span
    )


def widen(parent_values, height, breadth):
    parent_rows, parent_cols, feature = parent_values.shape
    spread_out = jnp.broadcast_to(
        parent_values[:, None, :, None, :], (parent_rows, 4, parent_cols, 4, feature)
    )
    return spread_out.reshape(height, breadth, feature)


def assemble_nodes(pieces, across, along):
    total, block_rows, block_cols, feature = pieces.shape
    arranged = pieces.reshape(across, along, block_rows, block_cols, feature).transpose(
        0, 2, 1, 3, 4
    )
    return arranged.reshape(across * block_rows, along * block_cols, feature)


def per_device(
    fine_nodes,
    fine_edges,
    fine_links,
    mid_nodes,
    mid_edges,
    mid_links,
    coarse_nodes,
    coarse_edges,
    coarse_links,
    edge_self,
    edge_sender,
    edge_receiver,
    edge_bias,
    edge_output,
    edge_gain,
    edge_shift,
    node_self,
    node_summed,
    node_bias,
    node_output,
    node_gain,
    node_shift,
    prolongation,
    pooling,
):
    tile_rows, tile_cols, feature = fine_nodes.shape
    mid_rows, mid_cols = (tile_rows // 4, tile_cols // 4)
    block_rows, block_cols = (tile_rows // 16, tile_cols // 16)
    coarse_rows, coarse_cols = (coarse_nodes.shape[0], coarse_nodes.shape[1])
    across = lax.axis_size("dx")
    along = lax.axis_size("dy")
    first_index = lax.axis_index("dx")
    second_index = lax.axis_index("dy")
    row_offset = first_index * block_rows
    col_offset = second_index * block_cols
    zero_offset = jnp.zeros((), jnp.int32)
    weights = tuple(
        (
            stacked[0]
            for stacked in (
                edge_self,
                edge_receiver,
                edge_bias,
                edge_output,
                edge_gain,
                edge_shift,
                node_self,
                node_summed,
                node_bias,
                node_output,
                node_gain,
                node_shift,
            )
        )
    )
    sender_matrix = edge_sender[0]
    fine_rim = with_halo(fine_nodes, (("dx", 0), ("dy", 1)), FINE_REACH)
    fine_terms = jnp.dot(
        fine_rim.reshape(-1, feature), sender_matrix, preferred_element_type=jnp.float32
    )
    fine_index = offset_index(fine_links, FINE_REACH, tile_cols + 2 * FINE_REACH)
    fine_new, fine_edges = level_update(fine_nodes, fine_edges, fine_terms, fine_index, weights)
    pooled = (
        mid_nodes.astype(jnp.float32)
        .reshape(block_rows, 4, block_cols, 4, feature)
        .mean(axis=(1, 3))
        .astype(jnp.bfloat16)
    )
    raised = jnp.dot(pooled.reshape(-1, feature), pooling[0], preferred_element_type=jnp.float32)
    own_coarse = lax.dynamic_slice(
        coarse_nodes, (row_offset, col_offset, zero_offset), (block_rows, block_cols, feature)
    )
    own_coarse = (
        own_coarse.astype(jnp.float32) + raised.reshape(block_rows, block_cols, feature)
    ).astype(jnp.bfloat16)
    gathered = lax.all_gather(own_coarse[None], ("dx", "dy"), axis=0, tiled=True)
    coarse_nodes = assemble_nodes(gathered, across, along)
    coarse_terms = jnp.dot(
        coarse_nodes.reshape(-1, feature), sender_matrix, preferred_element_type=jnp.float32
    )
    coarse_nodes, coarse_edges = level_update(
        coarse_nodes, coarse_edges, coarse_terms, coarse_links, weights
    )
    lifted = jnp.dot(
        coarse_nodes.reshape(-1, feature), prolongation[0], preferred_element_type=jnp.float32
    )
    lifted = lifted.reshape(coarse_rows, coarse_cols, feature)
    own_lift = lax.dynamic_slice(
        lifted, (row_offset, col_offset, zero_offset), (block_rows, block_cols, feature)
    )
    mid_nodes = (mid_nodes.astype(jnp.float32) + widen(own_lift, mid_rows, mid_cols)).astype(
        jnp.bfloat16
    )
    mid_source = mid_nodes
    mid_rim = with_halo(mid_source, (("dx", 0), ("dy", 1)), MID_REACH)
    mid_terms = jnp.dot(
        mid_rim.reshape(-1, feature), sender_matrix, preferred_element_type=jnp.float32
    )
    mid_index = offset_index(mid_links, MID_REACH, mid_cols + 2 * MID_REACH)
    mid_nodes, mid_edges = level_update(mid_nodes, mid_edges, mid_terms, mid_index, weights)
    lifted_mid = jnp.dot(
        mid_nodes.reshape(-1, feature), prolongation[0], preferred_element_type=jnp.float32
    )
    lifted_mid = lifted_mid.reshape(mid_rows, mid_cols, feature)
    fine_nodes = (fine_new.astype(jnp.float32) + widen(lifted_mid, tile_rows, tile_cols)).astype(
        jnp.bfloat16
    )
    return (fine_nodes, fine_edges, mid_nodes, mid_edges, coarse_nodes, coarse_edges)


def solution(mesh):
    placed = (
        P("dx", "dy", None),
        P(None, "dx", "dy", None),
        P(None, "dx", "dy"),
        P("dx", "dy", None),
        P(None, "dx", "dy", None),
        P(None, "dx", "dy"),
        P(),
        P(),
        P(),
        P(),
        P(),
        P(),
        P(),
        P(),
        P(),
        P(),
        P(),
        P(),
        P(),
        P(),
        P(),
        P(),
        P(),
        P(),
    )
    return jax.shard_map(
        per_device,
        mesh=mesh,
        in_specs=placed,
        out_specs=(
            P("dx", "dy", None),
            P(None, "dx", "dy", None),
            P("dx", "dy", None),
            P(None, "dx", "dy", None),
            P(),
            P(),
        ),
        check_vma=False,
    )
```

profile of v0, /device:TPU:0, one launch (start us, length us, event | category | flops | bytes accessed | tf_op | source)
XLA Modules:
  0.0 202.1 jit_solution(3112111262328539966)
XLA Ops:
  2.3 3.0 %collective-permute-start = (bf16[3,16,512]{2,1,0:T(8,128)(2,1)}, bf16[3,16,512]{2,1,0:T(8,128)(2,1)}, u32[]{:S(2)}, u32[]{:S(2)}) collective-permute-start(bf16[3,16,512]{2,1,0:T(8,128)(2,1)} %get-tuple-element.9), channel_id=1, source_target_pairs={{0,8},{8,16},{16,24},{24,0},{1,9},{9,17},{17,25},{25,1},{2,10},{10... | collective-permute-start | bytes 147464 | tf_op jit(solution)/shard_map/ppermute | solution.py:20
  12.1 41.9 %all-gather = bf16[64,1,512]{2,1,0:T(2,128)(2,1)S(1)} all-gather(bf16[2,1,512]{2,1,0:T(2,128)(2,1)S(1)} %copy.63), channel_id=2, replica_groups=mesh['dx'=4,'dy'=8] {'dx','dy'}, dimensions={0}, use_global_device_ids=true | all-gather | bytes 67584 | tf_op jit(solution)/shard_map/all_gather | solution.py:184
  59.7 3.0 %gather_fusion.1 = f32[384,1536]{1,0:T(8,128)} fusion(f32[64,1536]{1,0:T(8,128)S(1)} %fusion.26, s32[1024]{0:T(1024)} %get-tuple-element.27), kind=kCustom, calls=%fused_computation.1 | custom fusion | bytes 4720128 | tf_op jit(solution)/shard_map/jit(_take)/gather | solution.py:57
  64.0 2.9 %multiply_convert_fusion.2 = bf16[6,64,1536]{2,1,0:T(8,128)(2,1)S(1)} fusion(f32[6,64,1536]{2,1,0:T(8,128)} %bitcast.163, bf16[1,512,1536]{2,1,0:T(8,128)(2,1)S(1)} %copy-done, f32[64,1536]{1,0:T(8,128)S(1)} %convolution_add_fusion.5, pred[6,64]{1,0:T(8,128)(4,1)S(1)} %copy-done.44, bf16[6,8,8,512]{3,2,1,0:T(8,128)(2,1)S(1)} %copy-done.21), kind=kOutput, calls=%fused_computation.15 | convolution fusion | flops 608698368 | bytes 5898624 | tf_op jit(solution)/shard_map/dot_general | solution.py:53
  71.6 2.8 %fusion.85 = (f32[64]{0:T(128)S(1)}, f32[64,512]{1,0:T(8,128)S(1)}) fusion(bf16[1,1536,512]{2,1,0:T(8,128)(2,1)} %param.43, f32[64,1536]{1,0:T(8,128)} %fusion.35, bf16[64,512]{1,0:T(8,128)(2,1)S(1)} %reduce_sum.170, bf16[1,512,1536]{2,1,0:T(8,128)(2,1)} %param.41, f32[1536]{0:T(1024)S(1)} %reduce.7), kind=kOutput, calls=%fused_computation.148 | convolution fusion | flops 202047424 | bytes 3741952 | tf_op jit(solution)/shard_map/dot_general | solution.py:71
  77.4 2.9 %collective-permute-start.5 = (bf16[1,4,512]{2,1,0:T(4,128)(2,1)}, bf16[1,4,512]{2,1,0:T(4,128)(2,1)}, u32[]{:S(2)}, u32[]{:S(2)}) collective-permute-start(bf16[1,4,512]{2,1,0:T(4,128)(2,1)} %get-tuple-element.13), channel_id=1, source_target_pairs={{8,0},{16,8},{24,16},{0,24},{9,1},{17,9},{25,17},{1,25},{10,2},{18... | collective-permute-start | bytes 12296 | tf_op jit(solution)/shard_map/ppermute | solution.py:21
  81.9 4.3 %convolution_add_fusion.1 = f32[512,1536]{1,0:T(8,128)} fusion(bf16[512,512]{1,0:T(8,128)(2,1)} %bitcast.160, bf16[1,512,1536]{2,1,0:T(8,128)(2,1)} %param.35, f32[1536]{0:T(1024)S(1)} %reduce.6), kind=kOutput, calls=%fused_computation.9 | convolution fusion | flops 806092800 | bytes 5249024 | tf_op jit(solution)/shard_map/dot_general | solution.py:52
  86.1 2.7 %fusion.37 = f32[512,1536]{1,0:T(8,128)} fusion(bf16[512,512]{1,0:T(8,128)(2,1)S(1)} %bitcast.161, bf16[1,512,1536]{2,1,0:T(8,128)(2,1)S(1)} %copy-done.2), kind=kOutput, calls=%fused_computation.53 | convolution fusion | flops 805306368 | bytes 5242880 | tf_op jit(solution)/shard_map/dot_general | solution.py:66
  88.9 2.5 %convolution_add_fusion.7 = f32[32,1536]{1,0:T(8,128)} fusion(bf16[32,512]{1,0:T(8,128)(2,1)S(1)} %reshape.307, bf16[1,512,1536]{2,1,0:T(8,128)(2,1)} %param.35, f32[1536]{0:T(1024)S(1)} %reduce.6), kind=kOutput, calls=%fused_computation.21 | convolution fusion | flops 50380800 | bytes 1808384 | tf_op jit(solution)/shard_map/dot_general | solution.py:52
  95.7 3.5 %collective-permute-start.7 = (bf16[10,1,512]{2,1,0:T(2,128)(2,1)S(1)}, bf16[10,1,512]{2,1,0:T(2,128)(2,1)S(1)}, u32[]{:S(2)}, u32[]{:S(2)}) collective-permute-start(bf16[10,1,512]{2,1,0:T(2,128)(2,1)S(1)} %get-tuple-element.11), channel_id=1, source_target_pairs={{1,0},{2,1},{3,2},{4,3},{5,4},{6,5},{7,6},{0,7},{9,8},{10,9},{11,1... | collective-permute-start | bytes 30728 | tf_op jit(solution)/shard_map/ppermute | solution.py:21
  105.9 2.0 %gather_fusion.2 = f32[192,1536]{1,0:T(8,128)} fusion(f32[60,1536]{1,0:T(8,128)S(1)} %fusion.24, s32[1024]{0:T(1024)S(1)} %copy-done.39), kind=kCustom, calls=%fused_computation.2 | custom fusion | bytes 2360064 | tf_op jit(solution)/shard_map/jit(_take)/gather | solution.py:57
  111.8 3.9 %fusion.89 = (f32[32]{0:T(128)}, f32[32,512]{1,0:T(8,128)}) fusion(bf16[1,1536,512]{2,1,0:T(8,128)(2,1)} %param.43, f32[32,1536]{1,0:T(8,128)S(1)} %copy-done.18, bf16[32,512]{1,0:T(8,128)(2,1)} %reduce_sum.175, bf16[1,512,1536]{2,1,0:T(8,128)(2,1)} %param.41, f32[1536]{0:T(1024)} %copy-done.28), kind=kOutput, calls=%fused_computation.150 | convolution fusion | flops 101023712 | bytes 3446912 | tf_op jit(solution)/shard_map/dot_general | solution.py:71
  122.8 3.5 %collective-permute-start.3 = (bf16[38,3,512]{2,1,0:T(4,128)(2,1)}, bf16[38,3,512]{2,1,0:T(4,128)(2,1)}, u32[]{:S(2)}, u32[]{:S(2)}) collective-permute-start(bf16[38,3,512]{2,1,0:T(4,128)(2,1)} %get-tuple-element.7), channel_id=1, source_target_pairs={{1,0},{2,1},{3,2},{4,3},{5,4},{6,5},{7,6},{0,7},{9,8},{10,9},{11,1... | collective-permute-start | bytes 350216 | tf_op jit(solution)/shard_map/ppermute | solution.py:21
  128.5 2.6 %reshape.314 = f32[32,16,512]{2,1,0:T(8,128)} reshape(f32[8,4,4,4,512]{4,3,2,1,0:T(4,128)} %broadcast_in_dim.76) | data formatting | bytes 2097152 | tf_op jit(solution)/shard_map/reshape | solution.py:97
  131.1 2.7 %pad_maximum_fusion = bf16[38,22,512]{2,1,0:T(8,128)(2,1)} fusion(bf16[38,3,512]{2,1,0:T(4,128)(2,1)} %collective-permute-done.3, bf16[38,16,512]{2,1,0:T(8,128)(2,1)} %copy-done.17, bf16[38,3,512]{2,1,0:T(4,128)(2,1)} %collective-permute-done.2), kind=kLoop, calls=%fused_computation.63 | loop fusion | flops 2568192 | bytes 1712128 | tf_op jit(solution)/shard_map/concatenate | solution.py:22
  133.7 2.1 %reshape.297 = bf16[836,512]{1,0:T(8,128)(2,1)} reshape(bf16[38,22,512]{2,1,0:T(8,128)(2,1)} %pad_maximum_fusion) | data formatting | bytes 1712128 | tf_op jit(solution)/shard_map/reshape | solution.py:167
  135.9 5.0 %fusion.28 = f32[836,1536]{1,0:T(8,128)} fusion(bf16[836,512]{1,0:T(8,128)(2,1)} %reshape.297, bf16[1,512,1536]{2,1,0:T(8,128)(2,1)S(1)} %copy-done.5), kind=kOutput, calls=%fused_computation.44 | convolution fusion | flops 1314914304 | bytes 7565312 | tf_op jit(solution)/shard_map/dot_general | solution.py:166
  140.9 23.1 %gather_fusion = f32[3072,1536]{1,0:T(8,128)} fusion(f32[836,1536]{1,0:T(8,128)} %fusion.28, s32[3072]{0:T(1024)S(1)} %broadcast_clamp_fusion), kind=kCustom, calls=%fused_computation | custom fusion | bytes 37761024 | tf_op jit(solution)/shard_map/jit(_take)/gather | solution.py:57
  164.0 14.7 %multiply_convert_fusion = bf16[6,512,1536]{2,1,0:T(8,128)(2,1)} fusion(f32[6,512,1536]{2,1,0:T(8,128)} %bitcast.157, f32[512,1536]{1,0:T(8,128)} %convolution_add_fusion.1, pred[6,512]{1,0:T(8,128)(4,1)S(1)} %copy-done.42, bf16[6,512,512]{2,1,0:T(8,128)(2,1)} %bitcast.162, bf16[1,512,1536]{2,1,0:T(8,128)(2,1)S(1)} %copy-done), kind=kOutput, calls=%fused_computation.3 | convolution fusion | flops 4869586944 | bytes 36178944 | tf_op jit(solution)/shard_map/dot_general | solution.py:53
  178.7 7.9 %fusion.92 = (f32[3072]{0:T(1024)S(1)}, f32[3072,512]{1,0:T(8,128)S(1)}) fusion(bf16[3072,1536]{1,0:T(8,128)(2,1)} %bitcast.187, bf16[1,1536,512]{2,1,0:T(8,128)(2,1)S(1)} %copy-done.14), kind=kOutput, calls=%fused_computation.151 | convolution fusion | flops 4833408000 | bytes 17313792 | tf_op jit(solution)/shard_map/dot_general | solution.py:60
  186.6 2.1 %multiply_reduce_fusion = f32[3072]{0:T(1024)S(1)} fusion(f32[3072,512]{1,0:T(8,128)S(1)} %get-tuple-element.23, f32[3072]{0:T(1024)S(1)} %broadcast_multiply_fusion), kind=kLoop, calls=%fused_computation.6 | loop fusion | flops 4715520 | bytes 6316032 | tf_op jit(solution)/shard_map/reduce_sum | solution.py:29
  188.8 3.0 %fusion = bf16[3072,512]{1,0:T(8,128)(2,1)} fusion(f32[3072,512]{1,0:T(8,128)S(1)} %get-tuple-element.23, bf16[6,32,16,512]{3,2,1,0:T(8,128)(2,1)S(1)} %copy-done.9, f32[512]{0:T(512)S(1)} %bitcast.176, f32[512]{0:T(512)S(1)} %bitcast.179, f32[3072]{0:T(1024)S(1)} %add_rsqrt_fusion, f32[3072]{0:T(1024)S(1)} %broadcast_multiply_fusion), kind=kLoop, calls=%fused_computation.5 | loop fusion | flops 11010048 | bytes 12611584 | tf_op jit(solution)/shard_map/convert_element_type | solution.py:61
  191.8 3.4 %reduce_sum.162 = bf16[512,512]{1,0:T(8,128)(2,1)} reduce(bf16[6,512,512]{2,1,0:T(8,128)(2,1)} %bitcast.158, bf16[]{:T(256)} %constant.133.clone.1), dimensions={0}, to_apply=%region_2.3 | reduce | flops 1310720 | bytes 3670018 | tf_op jit(solution)/shard_map/reduce_sum | solution.py:65
  195.2 4.7 %fusion.93 = (f32[512]{0:T(512)S(1)}, f32[512,512]{1,0:T(8,128)S(1)}) fusion(bf16[1,1536,512]{2,1,0:T(8,128)(2,1)S(1)} %copy-done.15, f32[512,1536]{1,0:T(8,128)} %fusion.37, bf16[512,512]{1,0:T(8,128)(2,1)} %reduce_sum.162, bf16[1,512,1536]{2,1,0:T(8,128)(2,1)} %param.41, f32[1536]{0:T(1024)S(1)} %copy-done.29), kind=kOutput, calls=%fused_computation.152 | convolution fusion | flops 1616379392 | bytes 7872512 | tf_op jit(solution)/shard_map/dot_general | solution.py:71
  (190 shorter events, 50.5 us)
Async XLA Ops:
  0.6 63.3 %copy-start = (bf16[1,512,1536]{2,1,0:T(8,128)(2,1)S(1)}, bf16[1,512,1536]{2,1,0:T(8,128)(2,1)}, u32[]{:S(2)}) copy-start(bf16[1,512,1536]{2,1,0:T(8,128)(2,1)} %param.33) | copy-start | bytes 4718596
  0.6 57.2 %copy-start.4 = (bf16[1,512,1536]{2,1,0:T(8,128)(2,1)S(1)}, bf16[1,512,1536]{2,1,0:T(8,128)(2,1)}, u32[]{:S(2)}) copy-start(bf16[1,512,1536]{2,1,0:T(8,128)(2,1)} %param.34) | copy-start | bytes 4718596
  2.3 116.1 %collective-permute-start = (bf16[3,16,512]{2,1,0:T(8,128)(2,1)}, bf16[3,16,512]{2,1,0:T(8,128)(2,1)}, u32[]{:S(2)}, u32[]{:S(2)}) collective-permute-start(bf16[3,16,512]{2,1,0:T(8,128)(2,1)} %get-tuple-element.9), channel_id=1, source_target_pairs={{0,8},{8,16},{16,24},{24,0},{1,9},{9,17},{17,25},{25,1},{2,10},{10... | collective-permute-start | bytes 147464 | tf_op jit(solution)/shard_map/ppermute | solution.py:20
  5.2 115.1 %collective-permute-start.1 = (bf16[3,16,512]{2,1,0:T(8,128)(2,1)}, bf16[3,16,512]{2,1,0:T(8,128)(2,1)}, u32[]{:S(2)}, u32[]{:S(2)}) collective-permute-start(bf16[3,16,512]{2,1,0:T(8,128)(2,1)} %get-tuple-element.8), channel_id=1, source_target_pairs={{8,0},{16,8},{24,16},{0,24},{9,1},{17,9},{25,17},{1,25},{10,2},{18... | collective-permute-start | bytes 147464 | tf_op jit(solution)/shard_map/ppermute | solution.py:21
  9.3 62.3 %copy-start.28 = (f32[1536]{0:T(1024)}, f32[1536]{0:T(1024)S(1)}, u32[]{:S(2)}) copy-start(f32[1536]{0:T(1024)S(1)} %reduce.7) | copy-start | bytes 18436
  71.6 5.2 %copy-start.25 = (bf16[8,4,512]{2,1,0:T(4,128)(2,1)S(1)}, bf16[8,4,512]{2,1,0:T(4,128)(2,1)}, u32[]{:S(2)}) copy-start(bf16[8,4,512]{2,1,0:T(4,128)(2,1)} %param.27) | copy-start | bytes 98308
  71.6 8.7 %copy-start.27 = (s32[6,32,16]{1,2,0:T(8,128)S(1)}, s32[6,32,16]{1,2,0:T(8,128)}, u32[]{:S(2)}) copy-start(s32[6,32,16]{1,2,0:T(8,128)} %param.26) | copy-start | bytes 36868
  76.7 12.1 %copy-start.19 = (bf16[8,4,512]{2,1,0:T(4,128)(2,1)}, bf16[8,4,512]{2,1,0:T(4,128)(2,1)S(1)}, u32[]{:S(2)}) copy-start(bf16[8,4,512]{2,1,0:T(4,128)(2,1)S(1)} %fusion.65) | copy-start | bytes 98308
  77.4 17.4 %collective-permute-start.4 = (bf16[1,4,512]{2,1,0:T(4,128)(2,1)}, bf16[1,4,512]{2,1,0:T(4,128)(2,1)S(1)}, u32[]{:S(2)}, u32[]{:S(2)}) collective-permute-start(bf16[1,4,512]{2,1,0:T(4,128)(2,1)} %get-tuple-element.12), channel_id=1, source_target_pairs={{0,8},{8,16},{16,24},{24,0},{1,9},{9,17},{17,25},{25,1},{2,10},{10... | collective-permute-start | bytes 12296 | tf_op jit(solution)/shard_map/ppermute | solution.py:20
  77.4 17.4 %collective-permute-start.5 = (bf16[1,4,512]{2,1,0:T(4,128)(2,1)}, bf16[1,4,512]{2,1,0:T(4,128)(2,1)}, u32[]{:S(2)}, u32[]{:S(2)}) collective-permute-start(bf16[1,4,512]{2,1,0:T(4,128)(2,1)} %get-tuple-element.13), channel_id=1, source_target_pairs={{8,0},{16,8},{24,16},{0,24},{9,1},{17,9},{25,17},{1,25},{10,2},{18... | collective-permute-start | bytes 12296 | tf_op jit(solution)/shard_map/ppermute | solution.py:21
  92.4 12.2 %copy-start.5 = (bf16[1,512,1536]{2,1,0:T(8,128)(2,1)S(1)}, bf16[1,512,1536]{2,1,0:T(8,128)(2,1)}, u32[]{:S(2)}) copy-start(bf16[1,512,1536]{2,1,0:T(8,128)(2,1)} %param.34) | copy-start | bytes 4718596
  94.7 4.5 %copy-start.40 = (bf16[1,4,512]{2,1,0:T(4,128)(2,1)}, bf16[1,4,512]{2,1,0:T(4,128)(2,1)S(1)}, u32[]{:S(2)}) copy-start(bf16[1,4,512]{2,1,0:T(4,128)(2,1)S(1)} %collective-permute-done.4) | copy-start | bytes 12292
  95.6 7.5 %collective-permute-start.6 = (bf16[10,1,512]{2,1,0:T(2,128)(2,1)S(1)}, bf16[10,1,512]{2,1,0:T(2,128)(2,1)S(1)}, u32[]{:S(2)}, u32[]{:S(2)}) collective-permute-start(bf16[10,1,512]{2,1,0:T(2,128)(2,1)S(1)} %get-tuple-element.10), channel_id=1, source_target_pairs={{0,1},{1,2},{2,3},{3,4},{4,5},{5,6},{6,7},{7,0},{8,9},{9,10},{10,1... | collective-permute-start | bytes 30728 | tf_op jit(solution)/shard_map/ppermute | solution.py:20
  95.7 7.5 %collective-permute-start.7 = (bf16[10,1,512]{2,1,0:T(2,128)(2,1)S(1)}, bf16[10,1,512]{2,1,0:T(2,128)(2,1)S(1)}, u32[]{:S(2)}, u32[]{:S(2)}) collective-permute-start(bf16[10,1,512]{2,1,0:T(2,128)(2,1)S(1)} %get-tuple-element.11), channel_id=1, source_target_pairs={{1,0},{2,1},{3,2},{4,3},{5,4},{6,5},{7,6},{0,7},{9,8},{10,9},{11,1... | collective-permute-start | bytes 30728 | tf_op jit(solution)/shard_map/ppermute | solution.py:21
  99.8 6.1 %copy-start.39 = (s32[1024]{0:T(1024)S(1)}, s32[1024]{0:T(1024)}, u32[]{:S(2)}) copy-start(s32[1024]{0:T(1024)} %get-tuple-element.26) | copy-start | bytes 12292
  118.3 10.2 %copy-start.24 = (bf16[8,4,512]{2,1,0:T(4,128)(2,1)}, bf16[8,4,512]{2,1,0:T(4,128)(2,1)S(1)}, u32[]{:S(2)}) copy-start(bf16[8,4,512]{2,1,0:T(4,128)(2,1)S(1)} %reshape.313) | copy-start | bytes 98308
  118.3 8.0 %copy-start.10 = (bf16[1,512,512]{2,1,0:T(8,128)(2,1)S(1)}, bf16[1,512,512]{2,1,0:T(8,128)(2,1)}, u32[]{:S(2)}) copy-start(bf16[1,512,512]{2,1,0:T(8,128)(2,1)} %param.46) | copy-start | bytes 1572868
  122.8 8.3 %collective-permute-start.2 = (bf16[38,3,512]{2,1,0:T(4,128)(2,1)}, bf16[38,3,512]{2,1,0:T(4,128)(2,1)}, u32[]{:S(2)}, u32[]{:S(2)}) collective-permute-start(bf16[38,3,512]{2,1,0:T(4,128)(2,1)} %get-tuple-element.6), channel_id=1, source_target_pairs={{0,1},{1,2},{2,3},{3,4},{4,5},{5,6},{6,7},{7,0},{8,9},{9,10},{10,1... | collective-permute-start | bytes 350216 | tf_op jit(solution)/shard_map/ppermute | solution.py:20
  122.8 8.3 %collective-permute-start.3 = (bf16[38,3,512]{2,1,0:T(4,128)(2,1)}, bf16[38,3,512]{2,1,0:T(4,128)(2,1)}, u32[]{:S(2)}, u32[]{:S(2)}) collective-permute-start(bf16[38,3,512]{2,1,0:T(4,128)(2,1)} %get-tuple-element.7), channel_id=1, source_target_pairs={{1,0},{2,1},{3,2},{4,3},{5,4},{6,5},{7,6},{0,7},{9,8},{10,9},{11,1... | collective-permute-start | bytes 350216 | tf_op jit(solution)/shard_map/ppermute | solution.py:21
  140.9 23.1 %copy-start.42 = (pred[6,512]{1,0:T(8,128)(4,1)S(1)}, pred[6,512]{1,0:T(8,128)(4,1)}, u32[]{:S(2)}) copy-start(pred[6,512]{1,0:T(8,128)(4,1)} %compare_and_fusion) | copy-start | bytes 9220
  164.0 14.7 %copy-start.14 = (bf16[1,1536,512]{2,1,0:T(8,128)(2,1)S(1)}, bf16[1,1536,512]{2,1,0:T(8,128)(2,1)}, u32[]{:S(2)}) copy-start(bf16[1,1536,512]{2,1,0:T(8,128)(2,1)} %param.37) | copy-start | bytes 4718596
  195.2 5.0 %copy-start.7 = (bf16[32,16,512]{2,1,0:T(8,128)(2,1)S(1)}, bf16[32,16,512]{2,1,0:T(8,128)(2,1)}, u32[]{:S(2)}) copy-start(bf16[32,16,512]{2,1,0:T(8,128)(2,1)} %param.24) | copy-start | bytes 1572868
  195.2 5.0 %copy-start.36 = (f32[1,512]{1,0:T(1,128)S(1)}, f32[1,512]{1,0:T(1,128)}, u32[]{:S(2)}) copy-start(f32[1,512]{1,0:T(1,128)} %param.45) | copy-start | bytes 6148
  195.2 5.0 %copy-start.38 = (f32[1,512]{1,0:T(1,128)S(1)}, f32[1,512]{1,0:T(1,128)}, u32[]{:S(2)}) copy-start(f32[1,512]{1,0:T(1,128)} %param.44) | copy-start | bytes 6148
  (29 other events, 59.3 us)
where the time goes:
time: 204 us; the launch traced here: 202 us
  matrix products  63.3 us (31%)
  local copies, waits for them, and re-layouts  54.3 us (27%)
  blocking collectives  41.9 us (21%)
  other arithmetic  27.3 us (13%)
  starting transfers between devices  14 us (7%)
    all_gather x1, blocking collectives, per_device(): lax.all_gather(own_coarse[None], ('dx', 'dy'), axis=0, tiled=True)  41.9 us
    gather x3, local copies, waits for them, and re-layouts, level_update(): jnp.take(sender_terms, senders.reshape(fanout, places), axis=0)  28.2 us
    dot_general x3, matrix products, level_update(): jnp.dot(flat_edges, self_matrix, preferred_element_type=jnp.float32)  19.6 us
    dot_general x3, matrix products, level_update(): jnp.dot(node_hidden, node_output, preferred_element_type=jnp.float32)  11.4 us
    ppermute x4, starting transfers between devices, with_halo(): after = lax.ppermute(leading, axis, down)  11 us
    dot_general x3, matrix products, level_update(): message = jnp.dot(hidden, edge_output, preferred_element_type=jnp.float32)  9.31 us
    dot_general x3, matrix products, level_update(): jnp.dot(flat_nodes, receiver_matrix, preferred_element_type=jnp.float32)  8.03 us
    reduce_sum x3, other arithmetic, level_update(): summed = jnp.sum(new_edges.astype(jnp.float32), axis=0).astype(jnp.bfloat16)  5.09 us
  transfers between devices with their start and end apart: 8, of which 0 were waited for; matrix products, arithmetic and copies ran while one was open for 34% of the time, Pallas kernels for 0%

commit v1 on v0

v1 whole, which is shorter than its diff:
```python
import functools

import jax
import jax.numpy as jnp
from jax import lax
from jax.experimental import pallas as pl
from jax.experimental.pallas import tpu as pltpu
from jax.sharding import PartitionSpec as P

FINE_REACH = 3
MID_REACH = 1
BLOCK = 4
epsilon = 1e-05
F32 = jnp.float32
BF16 = jnp.bfloat16


def round_up(value, unit):
    return -(-value // unit) * unit


def exchange_kernel(
    across, along, x_ref, mid_ref, pad_ref, midpad_ref, pooled_ref,
    to_left, to_right, corner_src, top, bottom, from_left, from_right, corner_dst,
    mid_rows_dst, mid_left, mid_right, mid_corner, own_pool, pools,
    near_send, near_recv, pool_send, pool_recv,
):
    rows, cols, feature = x_ref.shape
    mrows, mcols, _ = mid_ref.shape
    half = rows // 2
    reach = FINE_REACH
    total = across * along
    me_x = lax.axis_index("dx")
    me_y = lax.axis_index("dy")
    me = me_x * along + me_y
    up = lax.rem(me_x + across - 1, across)
    down = lax.rem(me_x + 1, across)
    left = lax.rem(me_y + along - 1, along)
    right = lax.rem(me_y + 1, along)

    def other(step):
        number = lax.rem(me + step, total)
        return number // along, lax.rem(number, along)

    barrier = pltpu.get_barrier_semaphore()

    def greet(step, carry):
        pl.semaphore_signal(barrier, inc=1, device_id=other(step), device_id_type=pl.DeviceIdType.MESH)
        return carry

    lax.fori_loop(1, total, greet, 0)

    mid = mid_ref[...].astype(F32)
    brows, bcols = mrows // 4, mcols // 4
    for i in range(brows):
        strip = jnp.sum(mid[4 * i : 4 * i + 4], axis=0)
        for j in range(bcols):
            own_pool[i * bcols + j : i * bcols + j + 1, :] = (
                jnp.sum(strip[4 * j : 4 * j + 4], axis=0, keepdims=True) * (1.0 / 16.0)
            ).astype(BF16).astype(F32)

    low = lax.broadcasted_iota(jnp.int32, (half, 8, feature), 1) < 4
    first_a = x_ref[0:half, 0:8].astype(F32)
    first_b = x_ref[half:rows, 0:8].astype(F32)
    to_left[...] = jnp.where(low, first_a, pltpu.roll(first_b, 4, 1)).astype(BF16)
    last_a = x_ref[0:half, cols - 8 : cols].astype(F32)
    last_b = x_ref[half:rows, cols - 8 : cols].astype(F32)
    to_right[...] = jnp.where(low, pltpu.roll(last_a, 4, 1), last_b).astype(BF16)
    corner_src[0] = x_ref[rows - reach : rows, cols - 8 : cols]
    corner_src[1] = x_ref[rows - reach : rows, 0:8]
    corner_src[2] = x_ref[0:reach, cols - 8 : cols]
    corner_src[3] = x_ref[0:reach, 0:8]

    pl.semaphore_wait(barrier, total - 1)

    def pool_copy(slot, target):
        return pltpu.make_async_remote_copy(
            src_ref=own_pool, dst_ref=pools.at[slot], send_sem=pool_send.at[slot],
            recv_sem=pool_recv.at[slot], device_id=target, device_id_type=pl.DeviceIdType.MESH,
        )

    def send_pool(step, carry):
        pool_copy(step, other(step)).start()
        return carry

    lax.fori_loop(1, total, send_pool, 0)

    plan = (
        (to_right, from_left, (me_x, right)),
        (to_left, from_right, (me_x, left)),
        (x_ref.at[pl.ds(rows - reach, reach)], top, (down, me_y)),
        (x_ref.at[pl.ds(0, reach)], bottom, (up, me_y)),
        (corner_src.at[0], corner_dst.at[0], (down, right)),
        (corner_src.at[1], corner_dst.at[1], (down, left)),
        (corner_src.at[2], corner_dst.at[2], (up, right)),
        (corner_src.at[3], corner_dst.at[3], (up, left)),
        (mid_ref, mid_left, (me_x, right)),
        (mid_ref, mid_right, (me_x, left)),
        (mid_ref.at[mrows - 1], mid_rows_dst.at[0], (down, me_y)),
        (mid_ref.at[0], mid_rows_dst.at[1], (up, me_y)),
        (mid_ref.at[mrows - 1], mid_corner.at[0], (down, right)),
        (mid_ref.at[mrows - 1], mid_corner.at[1], (down, left)),
        (mid_ref.at[0], mid_corner.at[2], (up, right)),
        (mid_ref.at[0], mid_corner.at[3], (up, left)),
    )
    copies = []
    for number, (source, target, device) in enumerate(plan):
        copy = pltpu.make_async_remote_copy(
            src_ref=source, dst_ref=target, send_sem=near_send.at[number],
            recv_sem=near_recv.at[number], device_id=device, device_id_type=pl.DeviceIdType.MESH,
        )
        copy.start()
        copies.append(copy)

    pad_ref[reach : reach + rows, 0:cols] = x_ref[...]
    pad_ref[rows + 2 * reach] = jnp.zeros((cols + 8, feature), BF16)
    midpad_ref[...] = jnp.zeros(midpad_ref.shape, F32)
    for i in range(mrows):
        midpad_ref[i * mcols : (i + 1) * mcols, :] = mid[i]

    for copy in copies:
        copy.wait()

    pad_ref[0:reach, 0:cols] = top[...]
    pad_ref[rows + reach : rows + 2 * reach, 0:cols] = bottom[...]
    fr = from_right[...].astype(F32)
    fl = from_left[...].astype(F32)
    pad_ref[reach : reach + half, cols : cols + 8] = jnp.where(low, fr, pltpu.roll(fl, 4, 1)).astype(BF16)
    pad_ref[reach + half : reach + rows, cols : cols + 8] = jnp.where(low, pltpu.roll(fr, 4, 1), fl).astype(BF16)
    low3 = lax.broadcasted_iota(jnp.int32, (reach, 8, feature), 1) < 4
    pad_ref[0:reach, cols : cols + 8] = jnp.where(
        low3, corner_dst[1].astype(F32), corner_dst[0].astype(F32)
    ).astype(BF16)
    pad_ref[rows + reach : rows + 2 * reach, cols : cols + 8] = jnp.where(
        low3, corner_dst[3].astype(F32), corner_dst[2].astype(F32)
    ).astype(BF16)

    base = mrows * mcols
    midpad_ref[base : base + mcols, :] = mid_rows_dst[0].astype(F32)
    midpad_ref[base + mcols : base + 2 * mcols, :] = mid_rows_dst[1].astype(F32)
    for side, (tile, above, below) in enumerate(((mid_left, 0, 2), (mid_right, 1, 3))):
        start = base + 2 * mcols + side * (mrows + 2) * mcols
        midpad_ref[start : start + mcols, :] = mid_corner[above].astype(F32)
        values = tile[...].astype(F32)
        for i in range(mrows):
            midpad_ref[start + (i + 1) * mcols : start + (i + 2) * mcols, :] = values[i]
        finish = start + (mrows + 1) * mcols
        midpad_ref[finish : finish + mcols, :] = mid_corner[below].astype(F32)

    def finish_pool(step, carry):
        pool_copy(step, other(step)).wait()
        return carry

    lax.fori_loop(1, total, finish_pool, 0)
    count = brows * bcols
    pooled_ref[0] = own_pool[...]
    pooled_ref[1:total] = pools[1:total]


def exchange(fine_nodes, mid_nodes):
    across, along = lax.axis_size("dx"), lax.axis_size("dy")
    rows, cols, feature = fine_nodes.shape
    mrows, mcols, _ = mid_nodes.shape
    total = across * along
    count = (mrows // 4) * (mcols // 4)
    mid_total = round_up(3 * (mrows + 2) * mcols, 128)
    vmem = pl.BlockSpec(memory_space=pltpu.VMEM)
    return pl.pallas_call(
        functools.partial(exchange_kernel, across, along),
        name="exchange",
        out_shape=(
            jax.ShapeDtypeStruct((rows + 2 * FINE_REACH + 1, cols + 8, feature), BF16),
            jax.ShapeDtypeStruct((mid_total, feature), F32),
            jax.ShapeDtypeStruct((total, count, feature), F32),
        ),
        in_specs=[vmem] * 2,
        out_specs=[vmem] * 3,
        scratch_shapes=[
            pltpu.VMEM((rows // 2, 8, feature), BF16),
            pltpu.VMEM((rows // 2, 8, feature), BF16),
            pltpu.VMEM((4, FINE_REACH, 8, feature), BF16),
            pltpu.VMEM((FINE_REACH, cols, feature), BF16),
            pltpu.VMEM((FINE_REACH, cols, feature), BF16),
            pltpu.VMEM((rows // 2, 8, feature), BF16),
            pltpu.VMEM((rows // 2, 8, feature), BF16),
            pltpu.VMEM((4, FINE_REACH, 8, feature), BF16),
            pltpu.VMEM((2, mcols, feature), BF16),
            pltpu.VMEM((mrows, mcols, feature), BF16),
            pltpu.VMEM((mrows, mcols, feature), BF16),
            pltpu.VMEM((4, mcols, feature), BF16),
            pltpu.VMEM((count, feature), F32),
            pltpu.VMEM((total, count, feature), F32),
            pltpu.SemaphoreType.DMA((16,)),
            pltpu.SemaphoreType.DMA((16,)),
            pltpu.SemaphoreType.DMA((total,)),
            pltpu.SemaphoreType.DMA((total,)),
        ],
        compiler_params=pltpu.CompilerParams(collective_id=0, has_side_effects=True),
    )(fine_nodes, mid_nodes)


def silu(values):
    half = values * 0.5
    return half + half * jnp.tanh(half)


def normalize(values, gain_term, shift_term):
    average = jnp.mean(values, axis=-1, keepdims=True)
    centred = values - average
    variance = jnp.mean(centred * centred, axis=-1, keepdims=True)
    return centred * lax.rsqrt(variance + epsilon) * gain_term + shift_term


def dot(a, b):
    return jnp.dot(a, b, preferred_element_type=F32)


def chosen(index_row, length, width):
    padded = index_row.shape[1]
    turned = jnp.transpose(jnp.broadcast_to(index_row, (128, padded)))[:length]
    lane = lax.broadcasted_iota(jnp.int32, (length, 128), 1)
    parts = [
        jnp.where(turned == lane + start, 1.0, 0.0).astype(BF16) for start in range(0, width, 128)
    ]
    return parts[0] if len(parts) == 1 else jnp.concatenate(parts, axis=1)


def update_kernel(
    fanout,
    idx_ref, idx_mid_ref, idx_coarse_ref, idx_parent_ref, idx_pool_ref,
    x_ref, e_ref, pad_ref, midpad_ref, mid_e_ref, pooled_ref, coarse_ref, coarse_e_ref,
    ws_ref, wsend_ref, wrec_ref, ebias_ref, wo_ref, egain_ref, eshift_ref,
    ns_ref, nsum_ref, nbias_ref, no_ref, ngain_ref, nshift_ref, prol_ref, pool_ref,
    x_out, e_out, mid_out, mid_e_out, coarse_out, coarse_e_out,
    terms, receivers, act, summed,
):
    step = pl.program_id(0)
    steps = pl.num_programs(0)
    hidden = ws_ref.shape[1]
    chunk = 512
    places, feature = x_ref.shape
    block = e_ref.shape[1]
    mid_places = mid_out.shape[0]
    coarse_places = coarse_ref.shape[0]

    def edge_stage(edges, pick, terms_of, receiver_of, reps):
        length = edges.shape[0]
        for start in range(0, hidden, chunk):
            cut = slice(start, start + chunk)
            z = dot(edges, ws_ref[:, cut]) + dot(pick, terms_of(cut))
            z = z.reshape(reps, length // reps, chunk) + receiver_of(cut)[None]
            act[0:length, cut] = silu(z.reshape(length, chunk)).astype(BF16)
        message = dot(act[0:length, :], wo_ref[...])
        return (edges.astype(F32) + normalize(message, egain_ref[...], eshift_ref[...])).astype(BF16)

    def total_of(new, reps):
        return jnp.sum(new.astype(F32).reshape(reps, new.shape[0] // reps, feature), axis=0).astype(BF16)

    def node_stage(nodes, incoming):
        z = dot(nodes, ns_ref[...]) + dot(incoming, nsum_ref[...]) + nbias_ref[...]
        message = dot(silu(z).astype(BF16), no_ref[...])
        return (nodes.astype(F32) + normalize(message, ngain_ref[...], nshift_ref[...])).astype(BF16)

    def small_level(nodes, sources, edges_ref, edges_out, index_ref):
        count = nodes.shape[0]
        term = dot(sources, wsend_ref[...]).astype(BF16)
        receiver = dot(nodes, wrec_ref[...]) + ebias_ref[...]
        length = fanout * count
        width = sources.shape[0]
        if length <= act.shape[0]:
            pick = chosen(index_ref[...], length, round_up(width, 128))[:, :width]
            new = edge_stage(edges_ref[...], pick, lambda cut: term[:, cut], lambda cut: receiver[:, cut], fanout)
            edges_out[...] = new
            incoming = total_of(new, fanout)
        else:
            acc = jnp.zeros((count, feature), F32)
            for k in range(fanout):
                span = slice(k * count, (k + 1) * count)
                pick = chosen(index_ref[:, span], count, round_up(width, 128))[:, :width]
                new = edge_stage(edges_ref[span, :], pick, lambda cut: term[:, cut], lambda cut: receiver[:, cut], 1)
                edges_out[span, :] = new
                acc = acc + new.astype(F32)
            incoming = acc.astype(BF16)
        return node_stage(nodes, incoming)

    @pl.when(step == 0)
    def _():
        place = chosen(idx_pool_ref[...], coarse_places, round_up(coarse_places, 128))[:, :coarse_places]
        pooled = dot(place, pooled_ref[...].astype(BF16)).astype(BF16)
        coarse_pre = (coarse_ref[...].astype(F32) + dot(pooled, pool_ref[...])).astype(BF16)
        coarse = small_level(coarse_pre, coarse_pre, coarse_e_ref, coarse_e_out, idx_coarse_ref)
        coarse_out[...] = coarse
        extent = midpad_ref.shape[0]
        pick = chosen(idx_parent_ref[...], extent, round_up(coarse_places, 128))[:, :coarse_places]
        parent = dot(pick, coarse).astype(BF16)
        mid_pre = (midpad_ref[...] + dot(parent, prol_ref[...])).astype(BF16)
        mid_out[...] = small_level(mid_pre[:mid_places], mid_pre, mid_e_ref, mid_e_out, idx_mid_ref)
        terms[...] = dot(pad_ref[...], wsend_ref[...]).astype(BF16)
        receivers[...] = dot(x_ref[...], wrec_ref[...]) + ebias_ref[...]

    window = round_up((BLOCK + 2 * FINE_REACH) * (pad_ref.shape[0] // (places // block * BLOCK + 2 * FINE_REACH + 1)), 256)
    stride = pad_ref.shape[0] // (places // block * BLOCK + 2 * FINE_REACH + 1)
    begin = pl.multiple_of(step * (BLOCK * stride), BLOCK * stride)
    here = pl.multiple_of(step * block, block)
    length = fanout * block
    pick = chosen(idx_ref[0], length, window)
    new = edge_stage(
        e_ref[...].reshape(length, feature), pick,
        lambda cut: terms[pl.ds(begin, window), cut],
        lambda cut: receivers[pl.ds(here, block), cut], fanout,
    )
    e_out[...] = new.reshape(fanout, block, feature)
    summed[pl.ds(here, block), :] = total_of(new, fanout)

    @pl.when(step == steps - 1)
    def _():
        cols = block // BLOCK
        part = 256
        for start in range(0, places, part):
            rows = slice(start, start + part)
            fresh = node_stage(x_ref[rows, :], summed[rows, :])
            number = lax.broadcasted_iota(jnp.int32, (part, mid_places), 0) + start
            lane = lax.broadcasted_iota(jnp.int32, (part, mid_places), 1)
            owner = (number // cols // 4) * (cols // 4) + (number % cols) // 4
            pick = jnp.where(owner == lane, 1.0, 0.0).astype(BF16)
            lifted = dot(dot(pick, mid_out[...]).astype(BF16), prol_ref[...])
            x_out[rows, :] = (fresh.astype(F32) + lifted).astype(BF16)


def per_device(
    fine_nodes, fine_edges, fine_links, mid_nodes, mid_edges, mid_links, coarse_nodes, coarse_edges,
    coarse_links, edge_self, edge_sender, edge_receiver, edge_bias, edge_output, edge_gain, edge_shift,
    node_self, node_summed, node_bias, node_output, node_gain, node_shift, prolongation, pooling,
):
    rows, cols, feature = fine_nodes.shape
    mrows, mcols, _ = mid_nodes.shape
    crows, ccols, _ = coarse_nodes.shape
    fanout = fine_edges.shape[0]
    across, along = lax.axis_size("dx"), lax.axis_size("dy")
    me_x, me_y = lax.axis_index("dx"), lax.axis_index("dy")
    brows, bcols = mrows // 4, mcols // 4
    places, mid_places, coarse_places = rows * cols, mrows * mcols, crows * ccols
    stride = cols + 8
    steps = rows // BLOCK
    block = BLOCK * cols
    iota = functools.partial(lax.broadcasted_iota, jnp.int32)

    pad, midpad, pooled = exchange(fine_nodes, mid_nodes)

    span = 2 * FINE_REACH + 1
    shape = fine_links.shape
    column = (iota(shape, 2) + fine_links % span + (stride - FINE_REACH)) % stride
    index = (iota(shape, 1) % BLOCK + fine_links // span) * stride + column
    index = index.reshape(fanout, steps, block).transpose(1, 0, 2).reshape(steps, 1, fanout * block)

    shape = mid_links.shape
    line = iota(shape, 1) + mid_links // 3 - 1
    column = iota(shape, 2) + mid_links % 3 - 1
    centre = jnp.where(
        line < 0, mid_places + column, jnp.where(line >= mrows, mid_places + mcols + column, line * mcols + column)
    )
    side = mid_places + 2 * mcols + (line + 1) * mcols
    mid_index = jnp.where(
        column < 0, side + mcols - 1, jnp.where(column >= mcols, side + (mrows + 2) * mcols, centre)
    ).reshape(1, fanout * mid_places)
    short = round_up(fanout * mid_places, 128) - fanout * mid_places
    mid_index = jnp.pad(mid_index, ((0, 0), (0, short)))

    extent = midpad.shape[0]
    row = iota((1, extent), 1)
    beside = row - mid_places - 2 * mcols
    deep = (mrows + 2) * mcols
    line = jnp.where(
        row < mid_places, row // mcols,
        jnp.where(row < mid_places + mcols, -1, jnp.where(beside < 0, mrows, (beside % deep) // mcols - 1)),
    )
    column = jnp.where(beside < 0, row % mcols, jnp.where(beside < deep, -1, mcols))
    line = (me_x * mrows + line + across * mrows) % (across * mrows)
    column = (me_y * mcols + column + along * mcols) % (along * mcols)
    parent_index = (line // 4) * ccols + column // 4

    wide = round_up(coarse_places, 128)
    row = iota((1, wide), 1)
    line, column = row // ccols, row % ccols
    sender = (line // brows) * along + column // bcols
    slot = (me_x * along + me_y - sender + 2 * across * along) % (across * along)
    pool_index = slot * (brows * bcols) + (line % brows) * bcols + column % bcols
    coarse_index = coarse_links.reshape(1, fanout * coarse_places)

    whole = lambda shape: pl.BlockSpec(shape, lambda i: (0,) * len(shape), pipeline_mode=pl.Buffered(1))
    operands = [
        (index, pl.BlockSpec((1, 1, fanout * block), lambda i: (i, 0, 0))),
        mid_index,
        coarse_index,
        parent_index,
        pool_index,
        fine_nodes.reshape(places, feature),
        (fine_edges.reshape(fanout, places, feature), pl.BlockSpec((fanout, block, feature), lambda i: (0, i, 0))),
        pad.reshape(-1, feature),
        midpad,
        mid_edges.reshape(fanout * mid_places, feature),
        pooled.reshape(coarse_places, feature),
        coarse_nodes.reshape(coarse_places, feature),
        coarse_edges.reshape(fanout * coarse_places, feature),
    ]
    operands += [
        stacked[0] if stacked.ndim == 3 else stacked
        for stacked in (
            edge_self, edge_sender, edge_receiver, edge_bias, edge_output, edge_gain, edge_shift,
            node_self, node_summed, node_bias, node_output, node_gain, node_shift, prolongation, pooling,
        )
    ]
    specs = [item[1] if isinstance(item, tuple) else whole(item.shape) for item in operands]
    values = [item[0] if isinstance(item, tuple) else item for item in operands]
    hidden = edge_self.shape[2]
    struct = lambda *shape: jax.ShapeDtypeStruct(shape, BF16)
    fixed = lambda shape: pl.BlockSpec(shape, lambda i: (0,) * len(shape))
    fine_out, fine_e, mid_out, mid_e, coarse_out, coarse_e = pl.pallas_call(
        functools.partial(update_kernel, fanout),
        name="update",
        grid=(steps,),
        in_specs=specs,
        out_shape=(
            struct(places, feature),
            struct(fanout, places, feature),
            struct(mid_places, feature),
            struct(fanout * mid_places, feature),
            struct(coarse_places, feature),
            struct(fanout * coarse_places, feature),
        ),
        out_specs=(
            fixed((places, feature)),
            pl.BlockSpec((fanout, block, feature), lambda i: (0, i, 0)),
            fixed((mid_places, feature)),
            fixed((fanout * mid_places, feature)),
            fixed((coarse_places, feature)),
            fixed((fanout * coarse_places, feature)),
        ),
        scratch_shapes=[
            pltpu.VMEM(((rows + 2 * FINE_REACH + 1) * stride, hidden), BF16),
            pltpu.VMEM((places, hidden), F32),
            pltpu.VMEM((fanout * block, hidden), BF16),
            pltpu.VMEM((places, feature), BF16),
        ],
        compiler_params=pltpu.CompilerParams(vmem_limit_bytes=60 * 1024 * 1024),
    )(*values)
    return (
        fine_out.reshape(fine_nodes.shape),
        fine_e.reshape(fine_edges.shape),
        mid_out.reshape(mid_nodes.shape),
        mid_e.reshape(mid_edges.shape),
        coarse_out.reshape(coarse_nodes.shape),
        coarse_e.reshape(coarse_edges.shape),
    )


def solution(mesh):
    tile = P("dx", "dy", None)
    edge_tile = P(None, "dx", "dy", None)
    link_tile = P(None, "dx", "dy")
    return jax.shard_map(
        per_device,
        mesh=mesh,
        in_specs=(tile, edge_tile, link_tile) * 2 + (P(),) * 18,
        out_specs=(tile, edge_tile, tile, edge_tile, P(), P()),
        check_vma=False,
    )
```

time: 204 us -> 68.4 us (0.34)
  matrix products: 63.3 us -> 0 us
  Pallas kernels: 0 us -> 55.7 us
  local copies, waits for them, and re-layouts: 54.3 us -> 9.4 us
  blocking collectives: 41.9 us -> 0 us
  other arithmetic: 27.3 us -> 2.25 us
  starting transfers between devices: 14 us -> 0 us
    dot_general x21 -> x0, matrix products: 63.3 us -> none  [the longest x3 19.6 us: level_update(): jnp.dot(flat_edges, self_matrix, preferred_element_type=jnp.float32)]
    pallas_call x0 -> x2, Pallas kernels: none -> 55.7 us  [the longest x1 37.4 us: per_device(): pl.pallas_call(functools.partial(update_kernel, fanout), name='update', g...]
    all_gather x1 -> x0, blocking collectives: 41.9 us -> none  [per_device(): lax.all_gather(own_coarse[None], ('dx', 'dy'), axis=0, tiled=True)]
    gather x3 -> x0, local copies, waits for them, and re-layouts: 28.2 us -> none  [level_update(): jnp.take(sender_terms, senders.reshape(fanout, places), axis=0)]
    ppermute x8 -> x0, starting transfers between devices: 14 us -> none  [the longest x4 11 us: with_halo(): after = lax.ppermute(leading, axis, down)]
    reduce_sum x11 -> x0, other arithmetic: 9.92 us -> none  [the longest x3 5.09 us: level_update(): summed = jnp.sum(new_edges.astype(jnp.float32), axis=0).astype(jnp.bfloat16)]
    convert_element_type x7 -> x0, other arithmetic: 6.42 us -> none  [the longest x3 4.19 us: level_update(): (flat_edges.astype(jnp.float32) + normalize(message, edge_gain, edge_shif...]
    unnamed x93 -> x0, local copies, waits for them, and re-layouts: 4.63 us -> none
  transfers between devices with their start and end apart: 8 -> 0, of which waited for: 0 -> 0; matrix products, arithmetic and copies ran while one was open for 34% -> 0% of each run, Pallas kernels for 0% -> 0%
where the time goes in v1:
time: 68.4 us; the launch traced here: 68 us
  Pallas kernels  55.7 us (81%)
  local copies, waits for them, and re-layouts  9.4 us (14%)
  other arithmetic  2.25 us (3%)
  between operations  0.69 us (1%)
    pallas_call x1, Pallas kernels, per_device(): pl.pallas_call(functools.partial(update_kernel, fanout), name='update', g...  37.4 us
    pallas_call x1, Pallas kernels, exchange(): pl.pallas_call(functools.partial(exchange_kernel, across, along), name='e...  18.3 us
    reshape x1, local copies, waits for them, and re-layouts, per_device(): mid_e.reshape(mid_edges.shape)  1.66 us
    reshape x1, local copies, waits for them, and re-layouts, per_device(): mid_edges.reshape(fanout * mid_places, feature)  1.65 us
    reshape x1, local copies, waits for them, and re-layouts, per_device(): pooled.reshape(coarse_places, feature)  1.63 us
    reshape x1, local copies, waits for them, and re-layouts, per_device(): coarse_index = coarse_links.reshape(1, fanout * coarse_places)  1.42 us
    reshape x1, local copies, waits for them, and re-layouts, per_device(): mid_out.reshape(mid_nodes.shape)  1.39 us

profile of v1, /device:TPU:0, one launch (start us, length us, event | category | flops | bytes accessed | tf_op | source)
XLA Modules:
  0.0 68.0 jit_solution(18012021503068820451)
XLA Ops:
  0.6 0.6 fusion.14
  1.3 1.4 %reshape.761.idx_coarse_ref = s32[1,384]{1,0:T(1,128)} reshape(s32[6,8,8]{2,1,0:T(8,128)} %param.32) | data formatting | bytes 3072 | tf_op jit(solution)/shard_map/reshape | solution.py:388
  2.7 0.8 %select_select_fusion = s32[6,8,4]{1,2,0:T(4,128)S(1)} fusion(s32[6,8,4]{1,2,0:T(4,128)} %param.29), kind=kLoop, calls=%fused_computation.16 | loop fusion | flops 5952 | bytes 1536 | tf_op jit(solution)/shard_map/jit(_where)/select_n | solution.py:363
  3.4 0.1 copy.33
  3.5 0.1 reshape.760
  3.6 0.6 pad.4.idx_mid_ref
  4.2 0.9 %fusion.2 = s32[6,32,16]{1,2,0:T(8,128)S(1)} fusion(s32[6,32,16]{1,2,0:T(8,128)} %param.26, s32[32]{0:T(128)S(1)} %get-tuple-element.24, s32[32]{0:T(128)S(1)} %get-tuple-element.25, pred[32]{0:T(512)(128)(4,1)S(1)} %compare_and_fusion), kind=kLoop, calls=%fused_computation.5 | loop fusion | flops 73728 | bytes 24864 | tf_op jit(solution)/shard_map/add | solution.py:353
  5.1 0.1 copy.31
  5.2 0.1 reshape.758
  5.3 0.7 %reshape.775.idx_ref = s32[8,1,384]{2,1,0:T(1,128)} reshape(s32[8,6,64]{2,1,0:T(8,128)S(1)} %copy.32) | data formatting | bytes 24576 | tf_op jit(solution)/shard_map/reshape | solution.py:354
  6.0 1.7 %reshape.765.mid_e_ref = bf16[192,512]{1,0:T(8,128)(2,1)} reshape(bf16[6,8,4,512]{3,2,1,0:T(4,128)(2,1)} %param.28) | data formatting | bytes 393216 | tf_op jit(solution)/shard_map/reshape | solution.py:401
  7.6 18.3 %exchange.1 = (bf16[39,24,512]{2,1,0:T(8,128)(2,1)}, f32[128,512]{1,0:T(8,128)}, f32[32,2,512]{2,1,0:T(2,128)}) custom-call(bf16[32,16,512]{2,1,0:T(8,128)(2,1)} %x_ref.1, bf16[8,4,512]{2,1,0:T(4,128)(2,1)} %mid_ref.1), custom_call_target="tpu_custom_call" | custom-call | tf_op jit(solution)/shard_map/exchange/pallas_call | solution.py:168
  26.0 1.6 %reshape.766.pooled_ref = f32[64,512]{1,0:T(8,128)} reshape(f32[32,2,512]{2,1,0:T(2,128)} %get-tuple-element.17) | data formatting | bytes 262144 | tf_op jit(solution)/shard_map/reshape | solution.py:402
  27.6 37.4 %update.1 = (bf16[512,512]{1,0:T(8,128)(2,1)}, bf16[6,512,512]{2,1,0:T(8,128)(2,1)}, bf16[32,512]{1,0:T(8,128)(2,1)}, bf16[192,512]{1,0:T(8,128)(2,1)}, bf16[64,...) custom-call(s32[8,1,384]{2,1,0:T(1,128)} %reshape.775.idx_ref, s32[1,256]{1,0:T(1,128)} %pad.4.idx_mid_ref, ...), custom_call_target="tpu_custom_call" | custom-call | tf_op jit(solution)/shard_map/update/pallas_call | solution.py:418
  65.0 1.4 %reshape.771 = bf16[8,4,512]{2,1,0:T(4,128)(2,1)} reshape(bf16[32,512]{1,0:T(8,128)(2,1)} %get-tuple-element.20) | data formatting | bytes 65536 | tf_op jit(solution)/shard_map/reshape | solution.py:450
  66.4 1.7 %reshape.772 = bf16[6,8,4,512]{3,2,1,0:T(4,128)(2,1)} reshape(bf16[192,512]{1,0:T(8,128)(2,1)} %get-tuple-element.21) | data formatting | bytes 393216 | tf_op jit(solution)/shard_map/reshape | solution.py:451
  (3 shorter events, 0.0 us)

commit v2 on v1

--- a/solution.py
+++ b/solution.py
@@ -22,7 +22,7 @@
 def exchange_kernel(
     across, along, x_ref, mid_ref, pad_ref, midpad_ref, pooled_ref,
     to_left, to_right, corner_src, top, bottom, from_left, from_right, corner_dst,
-    mid_rows_dst, mid_left, mid_right, mid_corner, own_pool, pools,
+    mid_src, mid_rows_dst, mid_left, mid_right, mid_corner, own_pool, pools,
     near_send, near_recv, pool_send, pool_recv,
 ):
     rows, cols, feature = x_ref.shape
@@ -52,12 +52,14 @@
 
     mid = mid_ref[...].astype(F32)
     brows, bcols = mrows // 4, mcols // 4
+    means = []
     for i in range(brows):
         strip = jnp.sum(mid[4 * i : 4 * i + 4], axis=0)
         for j in range(bcols):
-            own_pool[i * bcols + j : i * bcols + j + 1, :] = (
-                jnp.sum(strip[4 * j : 4 * j + 4], axis=0, keepdims=True) * (1.0 / 16.0)
-            ).astype(BF16).astype(F32)
+            means.append(jnp.sum(strip[4 * j : 4 * j + 4], axis=0, keepdims=True) * (1.0 / 16.0))
+    own_pool[...] = jnp.concatenate(means, axis=0).astype(BF16)
+    mid_src[0] = jnp.concatenate([mid[i, mcols - 1 : mcols] for i in range(mrows)], axis=0).astype(BF16)
+    mid_src[1] = jnp.concatenate([mid[i, 0:1] for i in range(mrows)], axis=0).astype(BF16)
 
     low = lax.broadcasted_iota(jnp.int32, (half, 8, feature), 1) < 4
     first_a = x_ref[0:half, 0:8].astype(F32)
@@ -94,8 +96,8 @@
         (corner_src.at[1], corner_dst.at[1], (down, left)),
         (corner_src.at[2], corner_dst.at[2], (up, right)),
         (corner_src.at[3], corner_dst.at[3], (up, left)),
-        (mid_ref, mid_left, (me_x, right)),
-        (mid_ref, mid_right, (me_x, left)),
+        (mid_src.at[0], mid_left, (me_x, right)),
+        (mid_src.at[1], mid_right, (me_x, left)),
         (mid_ref.at[mrows - 1], mid_rows_dst.at[0], (down, me_y)),
         (mid_ref.at[0], mid_rows_dst.at[1], (up, me_y)),
         (mid_ref.at[mrows - 1], mid_corner.at[0], (down, right)),
@@ -138,12 +140,13 @@
     base = mrows * mcols
     midpad_ref[base : base + mcols, :] = mid_rows_dst[0].astype(F32)
     midpad_ref[base + mcols : base + 2 * mcols, :] = mid_rows_dst[1].astype(F32)
-    for side, (tile, above, below) in enumerate(((mid_left, 0, 2), (mid_right, 1, 3))):
+    for side, (tile, above, below, seat) in enumerate(((mid_left, 0, 2, mcols - 1), (mid_right, 1, 3, 0))):
         start = base + 2 * mcols + side * (mrows + 2) * mcols
         midpad_ref[start : start + mcols, :] = mid_corner[above].astype(F32)
         values = tile[...].astype(F32)
         for i in range(mrows):
-            midpad_ref[start + (i + 1) * mcols : start + (i + 2) * mcols, :] = values[i]
+            place = start + (i + 1) * mcols + seat
+            midpad_ref[place : place + 1, :] = values[i : i + 1]
         finish = start + (mrows + 1) * mcols
         midpad_ref[finish : finish + mcols, :] = mid_corner[below].astype(F32)
 
@@ -153,8 +156,9 @@
 
     lax.fori_loop(1, total, finish_pool, 0)
     count = brows * bcols
-    pooled_ref[0] = own_pool[...]
-    pooled_ref[1:total] = pools[1:total]
+    pooled_ref[0:count, :] = own_pool[...].astype(F32)
+    for slot in range(1, total):
+        pooled_ref[slot * count : (slot + 1) * count, :] = pools[slot].astype(F32)
 
 
 def exchange(fine_nodes, mid_nodes):
@@ -171,7 +175,7 @@
         out_shape=(
             jax.ShapeDtypeStruct((rows + 2 * FINE_REACH + 1, cols + 8, feature), BF16),
             jax.ShapeDtypeStruct((mid_total, feature), F32),
-            jax.ShapeDtypeStruct((total, count, feature), F32),
+            jax.ShapeDtypeStruct((total * count, feature), F32),
         ),
         in_specs=[vmem] * 2,
         out_specs=[vmem] * 3,
@@ -184,12 +188,13 @@
             pltpu.VMEM((rows // 2, 8, feature), BF16),
             pltpu.VMEM((rows // 2, 8, feature), BF16),
             pltpu.VMEM((4, FINE_REACH, 8, feature), BF16),
+            pltpu.VMEM((2, mrows, feature), BF16),
             pltpu.VMEM((2, mcols, feature), BF16),
-            pltpu.VMEM((mrows, mcols, feature), BF16),
-            pltpu.VMEM((mrows, mcols, feature), BF16),
+            pltpu.VMEM((mrows, feature), BF16),
+            pltpu.VMEM((mrows, feature), BF16),
             pltpu.VMEM((4, mcols, feature), BF16),
-            pltpu.VMEM((count, feature), F32),
-            pltpu.VMEM((total, count, feature), F32),
+            pltpu.VMEM((count, feature), BF16),
+            pltpu.VMEM((total, count, feature), BF16),
             pltpu.SemaphoreType.DMA((16,)),
             pltpu.SemaphoreType.DMA((16,)),
             pltpu.SemaphoreType.DMA((total,)),
@@ -215,24 +220,30 @@
     return jnp.dot(a, b, preferred_element_type=F32)
 
 
-def chosen(index_row, length, width):
-    padded = index_row.shape[1]
-    turned = jnp.transpose(jnp.broadcast_to(index_row, (128, padded)))[:length]
-    lane = lax.broadcasted_iota(jnp.int32, (length, 128), 1)
-    parts = [
-        jnp.where(turned == lane + start, 1.0, 0.0).astype(BF16) for start in range(0, width, 128)
-    ]
-    return parts[0] if len(parts) == 1 else jnp.concatenate(parts, axis=1)
+def spread(values, length):
+    lines, width = values.shape
+    row = lax.broadcasted_iota(jnp.int32, (length, lines), 0)
+    line = lax.broadcasted_iota(jnp.int32, (length, lines), 1) * width
+    owner = jnp.where((row >= line) & (row < line + width), 1.0, 0.0).astype(BF16)
+    rows = dot(owner, values.astype(BF16))
+    row = lax.broadcasted_iota(jnp.int32, (length, width), 0)
+    lane = lax.broadcasted_iota(jnp.int32, (length, width), 1)
+    return jnp.sum(jnp.where(lax.rem(row, width) == lane, rows, 0.0), axis=1, keepdims=True)
+
+
+def chosen(column, width):
+    lane = lax.broadcasted_iota(jnp.int32, (column.shape[0], width), 1).astype(column.dtype)
+    return jnp.where(column == lane, 1.0, 0.0).astype(BF16)
 
 
 def update_kernel(
-    fanout,
-    idx_ref, idx_mid_ref, idx_coarse_ref, idx_parent_ref, idx_pool_ref,
+    fanout, across, along,
+    links_ref, mid_links_ref, coarse_links_ref,
     x_ref, e_ref, pad_ref, midpad_ref, mid_e_ref, pooled_ref, coarse_ref, coarse_e_ref,
     ws_ref, wsend_ref, wrec_ref, ebias_ref, wo_ref, egain_ref, eshift_ref,
     ns_ref, nsum_ref, nbias_ref, no_ref, ngain_ref, nshift_ref, prol_ref, pool_ref,
     x_out, e_out, mid_out, mid_e_out, coarse_out, coarse_e_out,
-    terms, receivers, act, summed,
+    terms, receivers, act, summed, codes, mid_flat, mid_new,
 ):
     step = pl.program_id(0)
     steps = pl.num_programs(0)
@@ -240,7 +251,11 @@
     chunk = 512
     places, feature = x_ref.shape
     block = e_ref.shape[1]
-    mid_places = mid_out.shape[0]
+    mrows, mcols, _ = mid_out.shape
+    mid_places = mrows * mcols
+    crows, ccols = coarse_links_ref.shape[0] // fanout, coarse_links_ref.shape[1]
+    lines, cols = links_ref.shape[0] // fanout, links_ref.shape[1]
+    stride = cols + 8
     coarse_places = coarse_ref.shape[0]
 
     def edge_stage(edges, pick, terms_of, receiver_of, reps):
@@ -261,49 +276,94 @@
         message = dot(silu(z).astype(BF16), no_ref[...])
         return (nodes.astype(F32) + normalize(message, ngain_ref[...], nshift_ref[...])).astype(BF16)
 
-    def small_level(nodes, sources, edges_ref, edges_out, index_ref):
+    def small_level(nodes, sources, edges_ref, edges_out, index):
         count = nodes.shape[0]
         term = dot(sources, wsend_ref[...]).astype(BF16)
         receiver = dot(nodes, wrec_ref[...]) + ebias_ref[...]
         length = fanout * count
         width = sources.shape[0]
         if length <= act.shape[0]:
-            pick = chosen(index_ref[...], length, round_up(width, 128))[:, :width]
-            new = edge_stage(edges_ref[...], pick, lambda cut: term[:, cut], lambda cut: receiver[:, cut], fanout)
-            edges_out[...] = new
+            pick = chosen(spread(index, length), width)
+            new = edge_stage(edges_ref[...].astype(BF16), pick, lambda cut: term[:, cut], lambda cut: receiver[:, cut], fanout)
+            edges_out[...] = new.astype(edges_out.dtype)
             incoming = total_of(new, fanout)
         else:
             acc = jnp.zeros((count, feature), F32)
             for k in range(fanout):
                 span = slice(k * count, (k + 1) * count)
-                pick = chosen(index_ref[:, span], count, round_up(width, 128))[:, :width]
-                new = edge_stage(edges_ref[span, :], pick, lambda cut: term[:, cut], lambda cut: receiver[:, cut], 1)
-                edges_out[span, :] = new
+                part = index.shape[0] // fanout
+                pick = chosen(spread(index[k * part : (k + 1) * part], count), width)
+                new = edge_stage(edges_ref[span, :].astype(BF16), pick, lambda cut: term[:, cut], lambda cut: receiver[:, cut], 1)
+                edges_out[span, :] = new.astype(edges_out.dtype)
                 acc = acc + new.astype(F32)
             incoming = acc.astype(BF16)
         return node_stage(nodes, incoming)
 
     @pl.when(step == 0)
     def _():
-        place = chosen(idx_pool_ref[...], coarse_places, round_up(coarse_places, 128))[:, :coarse_places]
+        me_x, me_y = lax.axis_index("dx"), lax.axis_index("dy")
+        brows, bcols = mrows // 4, mcols // 4
+        div, rem = lax.div, lax.rem
+        row = lax.broadcasted_iota(jnp.int32, (coarse_places, 1), 0)
+        line, column = div(row, ccols), rem(row, ccols)
+        slot = rem(me_x * along + me_y + across * along - div(line, brows) * along - div(column, bcols), across * along)
+        place = chosen(slot * (brows * bcols) + rem(line, brows) * bcols + rem(column, bcols), coarse_places)
         pooled = dot(place, pooled_ref[...].astype(BF16)).astype(BF16)
         coarse_pre = (coarse_ref[...].astype(F32) + dot(pooled, pool_ref[...])).astype(BF16)
-        coarse = small_level(coarse_pre, coarse_pre, coarse_e_ref, coarse_e_out, idx_coarse_ref)
+        coarse = small_level(coarse_pre, coarse_pre, coarse_e_ref, coarse_e_out, coarse_links_ref[...].astype(F32))
         coarse_out[...] = coarse
-        extent = midpad_ref.shape[0]
-        pick = chosen(idx_parent_ref[...], extent, round_up(coarse_places, 128))[:, :coarse_places]
-        parent = dot(pick, coarse).astype(BF16)
+
+        row = lax.broadcasted_iota(jnp.int32, (midpad_ref.shape[0], 1), 0)
+        beside = row - mid_places - 2 * mcols
+        deep = (mrows + 2) * mcols
+        seat = jnp.maximum(beside, 0)
+        line = jnp.where(
+            row < mid_places, div(row, mcols),
+            jnp.where(row < mid_places + mcols, -1, jnp.where(beside < 0, mrows, div(rem(seat, deep), mcols) - 1)),
+        )
+        column = jnp.where(beside < 0, rem(row, mcols), jnp.where(beside < deep, -1, mcols))
+        line = rem(me_x * mrows + line + across * mrows, across * mrows)
+        column = rem(me_y * mcols + column + along * mcols, along * mcols)
+        parent = dot(chosen(div(line, 4) * ccols + div(column, 4), coarse_places), coarse).astype(BF16)
         mid_pre = (midpad_ref[...] + dot(parent, prol_ref[...])).astype(BF16)
-        mid_out[...] = small_level(mid_pre[:mid_places], mid_pre, mid_e_ref, mid_e_out, idx_mid_ref)
+
+        links = mid_links_ref[...]
+        line = rem(lax.broadcasted_iota(jnp.int32, links.shape, 0), mrows) + div(links, 3) - 1
+        column = lax.broadcasted_iota(jnp.int32, links.shape, 1) + rem(links, 3) - 1
+        centre = jnp.where(
+            line < 0, mid_places + column,
+            jnp.where(line >= mrows, mid_places + mcols + column, line * mcols + column),
+        )
+        side = mid_places + 2 * mcols + (line + 1) * mcols
+        index = jnp.where(
+            column < 0, side + mcols - 1, jnp.where(column >= mcols, side + (mrows + 2) * mcols, centre)
+        )
+        for i in range(fanout * mrows):
+            mid_flat[i * mcols : (i + 1) * mcols, :] = mid_e_ref[i].astype(F32)
+        fresh = small_level(mid_pre[:mid_places], mid_pre, mid_flat, mid_flat, index.astype(F32))
+        for i in range(fanout * mrows):
+            mid_e_out[i] = mid_flat[i * mcols : (i + 1) * mcols, :].astype(BF16)
+        mid_new[...] = fresh
+        fresh = fresh.astype(F32)
+        for i in range(mrows):
+            mid_out[i] = fresh[i * mcols : (i + 1) * mcols].astype(BF16)
+
+        links = links_ref[...]
+        span = 2 * FINE_REACH + 1
+        column = lax.broadcasted_iota(jnp.int32, links.shape, 1) + rem(links, span) + (stride - FINE_REACH)
+        line = rem(lax.broadcasted_iota(jnp.int32, links.shape, 0), BLOCK) + div(links, span)
+        index = (line * stride + rem(column, stride)).astype(F32)
+        for k in range(fanout):
+            for i in range(lines // BLOCK):
+                codes[i, k * BLOCK : (k + 1) * BLOCK, :] = index[k * lines + i * BLOCK : k * lines + (i + 1) * BLOCK]
         terms[...] = dot(pad_ref[...], wsend_ref[...]).astype(BF16)
         receivers[...] = dot(x_ref[...], wrec_ref[...]) + ebias_ref[...]
 
-    window = round_up((BLOCK + 2 * FINE_REACH) * (pad_ref.shape[0] // (places // block * BLOCK + 2 * FINE_REACH + 1)), 256)
-    stride = pad_ref.shape[0] // (places // block * BLOCK + 2 * FINE_REACH + 1)
+    window = round_up((BLOCK + 2 * FINE_REACH) * stride, 256)
     begin = pl.multiple_of(step * (BLOCK * stride), BLOCK * stride)
     here = pl.multiple_of(step * block, block)
     length = fanout * block
-    pick = chosen(idx_ref[0], length, window)
+    pick = chosen(spread(codes[step], length), window)
     new = edge_stage(
         e_ref[...].reshape(length, feature), pick,
         lambda cut: terms[pl.ds(begin, window), cut],
@@ -314,7 +374,6 @@
 
     @pl.when(step == steps - 1)
     def _():
-        cols = block // BLOCK
         part = 256
         for start in range(0, places, part):
             rows = slice(start, start + part)
@@ -323,7 +382,7 @@
             lane = lax.broadcasted_iota(jnp.int32, (part, mid_places), 1)
             owner = (number // cols // 4) * (cols // 4) + (number % cols) // 4
             pick = jnp.where(owner == lane, 1.0, 0.0).astype(BF16)
-            lifted = dot(dot(pick, mid_out[...]).astype(BF16), prol_ref[...])
+            lifted = dot(dot(pick, mid_new[...]).astype(BF16), prol_ref[...])
             x_out[rows, :] = (fresh.astype(F32) + lifted).astype(BF16)
 
 
@@ -337,69 +396,23 @@
     crows, ccols, _ = coarse_nodes.shape
     fanout = fine_edges.shape[0]
     across, along = lax.axis_size("dx"), lax.axis_size("dy")
-    me_x, me_y = lax.axis_index("dx"), lax.axis_index("dy")
-    brows, bcols = mrows // 4, mcols // 4
     places, mid_places, coarse_places = rows * cols, mrows * mcols, crows * ccols
     stride = cols + 8
     steps = rows // BLOCK
     block = BLOCK * cols
-    iota = functools.partial(lax.broadcasted_iota, jnp.int32)
-
     pad, midpad, pooled = exchange(fine_nodes, mid_nodes)
-
-    span = 2 * FINE_REACH + 1
-    shape = fine_links.shape
-    column = (iota(shape, 2) + fine_links % span + (stride - FINE_REACH)) % stride
-    index = (iota(shape, 1) % BLOCK + fine_links // span) * stride + column
-    index = index.reshape(fanout, steps, block).transpose(1, 0, 2).reshape(steps, 1, fanout * block)
-
-    shape = mid_links.shape
-    line = iota(shape, 1) + mid_links // 3 - 1
-    column = iota(shape, 2) + mid_links % 3 - 1
-    centre = jnp.where(
-        line < 0, mid_places + column, jnp.where(line >= mrows, mid_places + mcols + column, line * mcols + column)
-    )
-    side = mid_places + 2 * mcols + (line + 1) * mcols
-    mid_index = jnp.where(
-        column < 0, side + mcols - 1, jnp.where(column >= mcols, side + (mrows + 2) * mcols, centre)
-    ).reshape(1, fanout * mid_places)
-    short = round_up(fanout * mid_places, 128) - fanout * mid_places
-    mid_index = jnp.pad(mid_index, ((0, 0), (0, short)))
-
-    extent = midpad.shape[0]
-    row = iota((1, extent), 1)
-    beside = row - mid_places - 2 * mcols
-    deep = (mrows + 2) * mcols
-    line = jnp.where(
-        row < mid_places, row // mcols,
-        jnp.where(row < mid_places + mcols, -1, jnp.where(beside < 0, mrows, (beside % deep) // mcols - 1)),
-    )
-    column = jnp.where(beside < 0, row % mcols, jnp.where(beside < deep, -1, mcols))
-    line = (me_x * mrows + line + across * mrows) % (across * mrows)
-    column = (me_y * mcols + column + along * mcols) % (along * mcols)
-    parent_index = (line // 4) * ccols + column // 4
-
-    wide = round_up(coarse_places, 128)
-    row = iota((1, wide), 1)
-    line, column = row // ccols, row % ccols
-    sender = (line // brows) * along + column // bcols
-    slot = (me_x * along + me_y - sender + 2 * across * along) % (across * along)
-    pool_index = slot * (brows * bcols) + (line % brows) * bcols + column % bcols
-    coarse_index = coarse_links.reshape(1, fanout * coarse_places)
 
     whole = lambda shape: pl.BlockSpec(shape, lambda i: (0,) * len(shape), pipeline_mode=pl.Buffered(1))
     operands = [
-        (index, pl.BlockSpec((1, 1, fanout * block), lambda i: (i, 0, 0))),
-        mid_index,
-        coarse_index,
-        parent_index,
-        pool_index,
+        fine_links.reshape(fanout * rows, cols),
+        mid_links.reshape(fanout * mrows, mcols),
+        coarse_links.reshape(fanout * crows, ccols),
         fine_nodes.reshape(places, feature),
         (fine_edges.reshape(fanout, places, feature), pl.BlockSpec((fanout, block, feature), lambda i: (0, i, 0))),
         pad.reshape(-1, feature),
         midpad,
-        mid_edges.reshape(fanout * mid_places, feature),
-        pooled.reshape(coarse_places, feature),
+        mid_edges.reshape(fanout * mrows, mcols, feature),
+        pooled,
         coarse_nodes.reshape(coarse_places, feature),
         coarse_edges.reshape(fanout * coarse_places, feature),
     ]
@@ -416,23 +429,23 @@
     struct = lambda *shape: jax.ShapeDtypeStruct(shape, BF16)
     fixed = lambda shape: pl.BlockSpec(shape, lambda i: (0,) * len(shape))
     fine_out, fine_e, mid_out, mid_e, coarse_out, coarse_e = pl.pallas_call(
-        functools.partial(update_kernel, fanout),
+        functools.partial(update_kernel, fanout, across, along),
         name="update",
         grid=(steps,),
         in_specs=specs,
         out_shape=(
             struct(places, feature),
             struct(fanout, places, feature),
-            struct(mid_places, feature),
-            struct(fanout * mid_places, feature),
+            struct(mrows, mcols, feature),
+            struct(fanout * mrows, mcols, feature),
             struct(coarse_places, feature),
             struct(fanout * coarse_places, feature),
         ),
         out_specs=(
             fixed((places, feature)),
             pl.BlockSpec((fanout, block, feature), lambda i: (0, i, 0)),
-            fixed((mid_places, feature)),
-            fixed((fanout * mid_places, feature)),
+            fixed((mrows, mcols, feature)),
+            fixed((fanout * mrows, mcols, feature)),
             fixed((coarse_places, feature)),
             fixed((fanout * coarse_places, feature)),
         ),
@@ -441,6 +454,9 @@
             pltpu.VMEM((places, hidden), F32),
             pltpu.VMEM((fanout * block, hidden), BF16),
             pltpu.VMEM((places, feature), BF16),
+            pltpu.VMEM((steps, fanout * BLOCK, cols), F32),
+            pltpu.VMEM((fanout * mid_places, feature), F32),
+            pltpu.VMEM((mid_places, feature), BF16),
         ],
         compiler_params=pltpu.CompilerParams(vmem_limit_bytes=60 * 1024 * 1024),
     )(*values)

time: 68.4 us -> 60 us (0.88)
  local copies, waits for them, and re-layouts: 9.4 us -> 2.96 us
  other arithmetic: 2.25 us -> 0 us
    reshape x8 -> x0, local copies, waits for them, and re-layouts: 8.62 us -> none  [the longest x1 1.66 us: per_device(): mid_e.reshape(mid_edges.shape)]
    unnamed x0 -> x2, local copies, waits for them, and re-layouts: none -> 2.96 us
    add x2 -> x0, other arithmetic: 1.5 us -> none  [the longest x1 0.89 us: per_device(): index = (iota(shape, 1) % BLOCK + fine_links // span) * stride + column]
    pallas_call x1, Pallas kernels: 37.4 us -> 38.8 us  [per_device(): pl.pallas_call(functools.partial(update_kernel, fanout, across, along), n...]
    pallas_call x1, Pallas kernels: 18.3 us -> 17.4 us  [exchange(): pl.pallas_call(functools.partial(exchange_kernel, across, along), name='e...]
    select_n x1 -> x0, other arithmetic: 0.75 us -> none  [per_device(): jnp.where(column < 0, side + mcols - 1, jnp.where(column >= mcols, side +...]
where the time goes in v2:
time: 60 us; the launch traced here: 59.7 us
  Pallas kernels  56.1 us (94%)
  local copies, waits for them, and re-layouts  2.96 us (5%)
  between operations  0.64 us (1%)
    pallas_call x1, Pallas kernels, per_device(): pl.pallas_call(functools.partial(update_kernel, fanout, across, along), n...  38.8 us
    pallas_call x1, Pallas kernels, exchange(): pl.pallas_call(functools.partial(exchange_kernel, across, along), name='e...  17.4 us
    unnamed x2, local copies, waits for them, and re-layouts  2.96 us

profile of v2, /device:TPU:0, one launch (start us, length us, event | category | flops | bytes accessed | tf_op | source)
XLA Modules:
  0.0 59.7 jit_solution(17011169594396321779)
XLA Ops:
  0.6 1.4 %copy.31 = s32[6,8,4]{2,1,0:T(8,128)} copy(s32[6,8,4]{1,2,0:T(4,128)} %param.29) | data formatting | bytes 1536 | tf_op args[5]
  2.1 1.5 %copy.30 = s32[6,32,16]{2,1,0:T(8,128)} copy(s32[6,32,16]{1,2,0:T(8,128)} %param.26) | data formatting | bytes 24576 | tf_op args[2]
  3.6 17.4 %exchange.1 = (bf16[39,24,512]{2,1,0:T(8,128)(2,1)}, f32[128,512]{1,0:T(8,128)}, f32[64,512]{1,0:T(8,128)}) custom-call(bf16[32,16,512]{2,1,0:T(8,128)(2,1)} %x_ref.1, bf16[8,4,512]{2,1,0:T(4,128)(2,1)} %mid_ref.1), custom_call_target="tpu_custom_call" | custom-call | tf_op jit(solution)/shard_map/exchange/pallas_call | solution.py:172
  21.0 38.8 %update.1 = (bf16[512,512]{1,0:T(8,128)(2,1)}, bf16[6,512,512]{2,1,0:T(8,128)(2,1)}, bf16[8,4,512]{2,1,0:T(4,128)(2,1)}, bf16[48,4,512]{2,1,0:T(4,128)(2,1)}, bf...) custom-call(s32[192,16]{1,0:T(8,128)} %bitcast.35, s32[48,4]{1,0:T(8,128)} %bitcast.38, s32[48,8]{1,0:T(8,128)} %bitcast.40, ...), custom_call_target="tpu_custom_call" | custom-call | tf_op jit(solution)/shard_map/update/pallas_call | solution.py:431

commit v3 on v2

--- a/solution.py
+++ b/solution.py
@@ -200,7 +200,10 @@
             pltpu.SemaphoreType.DMA((total,)),
             pltpu.SemaphoreType.DMA((total,)),
         ],
-        compiler_params=pltpu.CompilerParams(collective_id=0, has_side_effects=True),
+        cost_estimate=pl.CostEstimate(flops=15_000_000_000, bytes_accessed=50_000_000, transcendentals=0),
+        compiler_params=pltpu.CompilerParams(
+            collective_id=0, has_side_effects=True, vmem_limit_bytes=12 * 1024 * 1024
+        ),
     )(fine_nodes, mid_nodes)
 
 
@@ -402,7 +405,7 @@
     block = BLOCK * cols
     pad, midpad, pooled = exchange(fine_nodes, mid_nodes)
 
-    whole = lambda shape: pl.BlockSpec(shape, lambda i: (0,) * len(shape), pipeline_mode=pl.Buffered(1))
+    whole = lambda shape: pl.BlockSpec(memory_space=pltpu.VMEM)
     operands = [
         fine_links.reshape(fanout * rows, cols),
         mid_links.reshape(fanout * mrows, mcols),
@@ -458,7 +461,7 @@
             pltpu.VMEM((fanout * mid_places, feature), F32),
             pltpu.VMEM((mid_places, feature), BF16),
         ],
-        compiler_params=pltpu.CompilerParams(vmem_limit_bytes=60 * 1024 * 1024),
+        compiler_params=pltpu.CompilerParams(vmem_limit_bytes=32 * 1024 * 1024),
     )(*values)
     return (
         fine_out.reshape(fine_nodes.shape),

time: 60 us -> 53.9 us (0.90)
  Pallas kernels: 56.1 us -> 49 us
  local copies, waits for them, and re-layouts: 2.96 us -> 3.6 us
    pallas_call x1, Pallas kernels: 38.8 us -> 33.3 us  [per_device(): pl.pallas_call(functools.partial(update_kernel, fanout, across, along), n...]
    pallas_call x1, Pallas kernels: 17.4 us -> 15.6 us  [exchange(): pl.pallas_call(functools.partial(exchange_kernel, across, along), name='e...]
    unnamed x2 -> x48, local copies, waits for them, and re-layouts: 2.96 us -> 3.6 us
where the time goes in v3:
time: 53.9 us; the launch traced here: 53.5 us
  Pallas kernels  49 us (91%)
  local copies, waits for them, and re-layouts  3.6 us (7%)
  between operations  0.96 us (2%)
    pallas_call x1, Pallas kernels, per_device(): pl.pallas_call(functools.partial(update_kernel, fanout, across, along), n...  33.3 us
    pallas_call x1, Pallas kernels, exchange(): pl.pallas_call(functools.partial(exchange_kernel, across, along), name='e...  15.6 us
    unnamed x48, local copies, waits for them, and re-layouts  3.6 us

profile of v3, /device:TPU:0, one launch (start us, length us, event | category | flops | bytes accessed | tf_op | source)
XLA Modules:
  0.0 53.5 jit_solution(15091076605677903327)
XLA Ops:
  0.6 0.8 %copy.31 = s32[6,8,4]{2,1,0:T(8,128)S(1)} copy(s32[6,8,4]{1,2,0:T(4,128)} %param.29) | data formatting | bytes 1536 | tf_op args[5]
  1.4 0.9 %copy.30 = s32[6,32,16]{2,1,0:T(8,128)S(1)} copy(s32[6,32,16]{1,2,0:T(8,128)} %param.26) | data formatting | bytes 24576 | tf_op args[2]
  2.3 0.0 copy-start.8
  2.3 1.0 %copy-done.8 = bf16[32,16,512]{2,1,0:T(8,128)(2,1)S(1)} copy-done((bf16[32,16,512]{2,1,0:T(8,128)(2,1)S(1)}, bf16[32,16,512]{2,1,0:T(8,128)(2,1)}, u32[]{:S(2)}) %copy-start.8) | copy-done | bytes 524312
  3.4 0.8 %copy-done.22 = bf16[8,4,512]{2,1,0:T(4,128)(2,1)S(1)} copy-done((bf16[8,4,512]{2,1,0:T(4,128)(2,1)S(1)}, bf16[8,4,512]{2,1,0:T(4,128)(2,1)}, u32[]{:S(2)}) %copy-start.22) | copy-done | bytes 32792
  4.1 0.0 copy-start.4
  4.2 0.0 copy-start.5
  4.2 0.0 copy-start.6
  4.2 0.0 copy-start.7
  4.2 0.0 copy-start.9
  4.2 0.0 copy-start.10
  4.2 0.0 copy-start.11
  4.2 0.0 copy-start.12
  4.2 0.0 copy-start.13
  4.3 0.0 copy-start.14
  4.3 0.0 copy-start.15
  4.3 0.0 copy-start.16
  4.3 0.0 copy-start.17
  4.3 0.0 copy-start.18
  4.3 0.0 copy-start.19
  4.3 0.0 copy-start.20
  4.3 0.0 copy-start.21
  4.3 15.6 %exchange.1 = (bf16[39,24,512]{2,1,0:T(8,128)(2,1)S(1)}, f32[128,512]{1,0:T(8,128)S(1)}, f32[64,512]{1,0:T(8,128)S(1)}) custom-call(bf16[32,16,512]{2,1,0:T(8,128)(2,1)S(1)} %copy-done.8, bf16[8,4,512]{2,1,0:T(4,128)(2,1)S(1)} %copy-done.22), custom_call_target="tpu_custom_call" | custom-call | flops 15000000512 | bytes 50000000 | tf_op jit(solution)/shard_map/exchange/pallas_call | solution.py:172
  20.2 33.3 %update.1 = (bf16[512,512]{1,0:T(8,128)(2,1)}, bf16[6,512,512]{2,1,0:T(8,128)(2,1)}, bf16[8,4,512]{2,1,0:T(4,128)(2,1)}, bf16[48,4,512]{2,1,0:T(4,128)(2,1)}, bf...) custom-call(s32[192,16]{1,0:T(8,128)S(1)} %bitcast.35, s32[48,4]{1,0:T(8,128)S(1)} %bitcast.38, s32[48,8]{1,0:T(8,128)S(1)} %bitcast.40, ...), custom_call_target="tpu_custom_call" | custom-call | tf_op jit(solution)/shard_map/update/pallas_call | solution.py:434
  (26 shorter events, 0.1 us)
Async XLA Ops:
  2.3 1.0 %copy-start.8 = (bf16[32,16,512]{2,1,0:T(8,128)(2,1)S(1)}, bf16[32,16,512]{2,1,0:T(8,128)(2,1)}, u32[]{:S(2)}) copy-start(bf16[32,16,512]{2,1,0:T(8,128)(2,1)} %x_ref.1) | copy-start | bytes 1572868
  3.4 0.8 %copy-start.22 = (bf16[8,4,512]{2,1,0:T(4,128)(2,1)S(1)}, bf16[8,4,512]{2,1,0:T(4,128)(2,1)}, u32[]{:S(2)}) copy-start(bf16[8,4,512]{2,1,0:T(4,128)(2,1)} %mid_ref.1) | copy-start | bytes 98308
  4.1 15.9 %copy-start = (bf16[6,32,16,512]{3,2,1,0:T(8,128)(2,1)S(1)}, bf16[6,32,16,512]{3,2,1,0:T(8,128)(2,1)}, u32[]{:S(2)}) copy-start(bf16[6,32,16,512]{3,2,1,0:T(8,128)(2,1)} %param.25) | copy-start | bytes 9437188
  4.1 15.9 %copy-start.1 = (bf16[1,512,1536]{2,1,0:T(8,128)(2,1)S(1)}, bf16[1,512,1536]{2,1,0:T(8,128)(2,1)}, u32[]{:S(2)}) copy-start(bf16[1,512,1536]{2,1,0:T(8,128)(2,1)} %param.33) | copy-start | bytes 4718596
  4.1 15.9 %copy-start.2 = (bf16[1,512,1536]{2,1,0:T(8,128)(2,1)S(1)}, bf16[1,512,1536]{2,1,0:T(8,128)(2,1)}, u32[]{:S(2)}) copy-start(bf16[1,512,1536]{2,1,0:T(8,128)(2,1)} %param.34) | copy-start | bytes 4718596
  4.1 15.9 %copy-start.3 = (bf16[1,512,1536]{2,1,0:T(8,128)(2,1)S(1)}, bf16[1,512,1536]{2,1,0:T(8,128)(2,1)}, u32[]{:S(2)}) copy-start(bf16[1,512,1536]{2,1,0:T(8,128)(2,1)} %param.35) | copy-start | bytes 4718596
  4.1 15.9 %copy-start.4 = (bf16[1,1536,512]{2,1,0:T(8,128)(2,1)S(1)}, bf16[1,1536,512]{2,1,0:T(8,128)(2,1)}, u32[]{:S(2)}) copy-start(bf16[1,1536,512]{2,1,0:T(8,128)(2,1)} %param.37) | copy-start | bytes 4718596
  4.2 15.9 %copy-start.5 = (bf16[1,512,1536]{2,1,0:T(8,128)(2,1)S(1)}, bf16[1,512,1536]{2,1,0:T(8,128)(2,1)}, u32[]{:S(2)}) copy-start(bf16[1,512,1536]{2,1,0:T(8,128)(2,1)} %param.40) | copy-start | bytes 4718596
  4.2 15.9 %copy-start.6 = (bf16[1,512,1536]{2,1,0:T(8,128)(2,1)S(1)}, bf16[1,512,1536]{2,1,0:T(8,128)(2,1)}, u32[]{:S(2)}) copy-start(bf16[1,512,1536]{2,1,0:T(8,128)(2,1)} %param.41) | copy-start | bytes 4718596
  4.2 15.9 %copy-start.7 = (bf16[1,1536,512]{2,1,0:T(8,128)(2,1)S(1)}, bf16[1,1536,512]{2,1,0:T(8,128)(2,1)}, u32[]{:S(2)}) copy-start(bf16[1,1536,512]{2,1,0:T(8,128)(2,1)} %param.43) | copy-start | bytes 4718596
  4.2 15.9 %copy-start.9 = (bf16[32,16,512]{2,1,0:T(8,128)(2,1)S(1)}, bf16[32,16,512]{2,1,0:T(8,128)(2,1)}, u32[]{:S(2)}) copy-start(bf16[32,16,512]{2,1,0:T(8,128)(2,1)} %x_ref.1) | copy-start | bytes 1572868
  4.2 15.9 %copy-start.10 = (bf16[1,512,512]{2,1,0:T(8,128)(2,1)S(1)}, bf16[1,512,512]{2,1,0:T(8,128)(2,1)}, u32[]{:S(2)}) copy-start(bf16[1,512,512]{2,1,0:T(8,128)(2,1)} %param.46) | copy-start | bytes 1572868
  4.2 15.9 %copy-start.11 = (bf16[1,512,512]{2,1,0:T(8,128)(2,1)S(1)}, bf16[1,512,512]{2,1,0:T(8,128)(2,1)}, u32[]{:S(2)}) copy-start(bf16[1,512,512]{2,1,0:T(8,128)(2,1)} %param.47) | copy-start | bytes 1572868
  4.2 15.9 %copy-start.12 = (bf16[6,8,8,512]{3,2,1,0:T(8,128)(2,1)S(1)}, bf16[6,8,8,512]{3,2,1,0:T(8,128)(2,1)}, u32[]{:S(2)}) copy-start(bf16[6,8,8,512]{3,2,1,0:T(8,128)(2,1)} %param.31) | copy-start | bytes 1179652
  4.2 15.9 %copy-start.13 = (bf16[6,8,4,512]{3,2,1,0:T(4,128)(2,1)S(1)}, bf16[6,8,4,512]{3,2,1,0:T(4,128)(2,1)}, u32[]{:S(2)}) copy-start(bf16[6,8,4,512]{3,2,1,0:T(4,128)(2,1)} %param.28) | copy-start | bytes 589828
  4.3 15.9 %copy-start.14 = (bf16[8,8,512]{2,1,0:T(8,128)(2,1)S(1)}, bf16[8,8,512]{2,1,0:T(8,128)(2,1)}, u32[]{:S(2)}) copy-start(bf16[8,8,512]{2,1,0:T(8,128)(2,1)} %param.30) | copy-start | bytes 196612
  4.3 15.9 %copy-start.15 = (s32[6,8,8]{2,1,0:T(8,128)S(1)}, s32[6,8,8]{2,1,0:T(8,128)}, u32[]{:S(2)}) copy-start(s32[6,8,8]{2,1,0:T(8,128)} %param.32) | copy-start | bytes 4612
  4.3 15.9 %copy-start.16 = (f32[1,1536]{1,0:T(1,128)S(1)}, f32[1,1536]{1,0:T(1,128)}, u32[]{:S(2)}) copy-start(f32[1,1536]{1,0:T(1,128)} %ebias_ref.1) | copy-start | bytes 18436
  4.3 15.9 %copy-start.17 = (f32[1,1536]{1,0:T(1,128)S(1)}, f32[1,1536]{1,0:T(1,128)}, u32[]{:S(2)}) copy-start(f32[1,1536]{1,0:T(1,128)} %nbias_ref.1) | copy-start | bytes 18436
  4.3 15.9 %copy-start.18 = (f32[1,512]{1,0:T(1,128)S(1)}, f32[1,512]{1,0:T(1,128)}, u32[]{:S(2)}) copy-start(f32[1,512]{1,0:T(1,128)} %egain_ref.1) | copy-start | bytes 6148
  4.3 15.9 %copy-start.19 = (f32[1,512]{1,0:T(1,128)S(1)}, f32[1,512]{1,0:T(1,128)}, u32[]{:S(2)}) copy-start(f32[1,512]{1,0:T(1,128)} %eshift_ref.1) | copy-start | bytes 6148
  4.3 15.9 %copy-start.20 = (f32[1,512]{1,0:T(1,128)S(1)}, f32[1,512]{1,0:T(1,128)}, u32[]{:S(2)}) copy-start(f32[1,512]{1,0:T(1,128)} %ngain_ref.1) | copy-start | bytes 6148
  4.3 15.9 %copy-start.21 = (f32[1,512]{1,0:T(1,128)S(1)}, f32[1,512]{1,0:T(1,128)}, u32[]{:S(2)}) copy-start(f32[1,512]{1,0:T(1,128)} %nshift_ref.1) | copy-start | bytes 6148
